TPU v7x, 32 devices: a whole 2x2x4 slice. The times are simulated.
32 devices in a mesh: mx: 8 (over z, core), my: 4 (over y, x).
Axes of the slice: x: 2, y: 2, z: 4, core: 2. Of those that a mesh axis runs over, the one named last changes fastest.
Arguments:
- features: bfloat16 [1024, 32, 512], P(('mx', 'my')), may hold values from -6 to 6
- coords: int32 [3, 1024], P(None, ('mx', 'my')), may hold values from 0 to 31, as said below
- counts: int32 [32], P(('mx', 'my')), may hold values from 16 to 32, as said below
- neighbours: int32 [6, 1024], P(None, ('mx', 'my')), may hold values from -1 to 1023, as said below
- fine_weights: bfloat16 [3, 32, 224], replicated, may hold values from -0.375 to 0.375
- down_weight: bfloat16 [2048, 256], replicated, may hold values from -0.25 to 0.25
- up_weight: bfloat16 [256, 2048], replicated, may hold values from -0.375 to 0.375
- norm_gain: float32 [256], replicated, may hold values from 0.1 to 1.9
- norm_bias: float32 [256], replicated, may hold values from -3 to 3
- coarse_weight: bfloat16 [6912, 256], P(None, 'my'), may hold values from -0.078125 to 0.078125
Outputs:
- fine_out: bfloat16 [1024, 32, 512], P(('mx', 'my'))
- coarse_out: bfloat16 [16, 8, 2, 256], P('mx', 'my')
Inputs may be any that keep to these rules, and one draw needn't show every extreme that they name: The live slots of a device are its first counts entries; some device is full in every draw. `coords`: the live blocks of the device with mx index i and my index j lie at z in [i * 4, (i + 1) * 4), y in [j * 4, (j + 1) * 4), x in [0, 4), distinct, in Morton order of their coordinates inside that region; slots that are not live hold 0. `neighbours`: A live block's entry is the slot of the live block one step away in that direction, or -1 if there is none; the relation is symmetric; slots that are not live hold -1.
All inputs are finite; a program needn't handle non-finite values.
Results may differ from a plain program's by a relative error of at most 0.0095.
Values may be sent and summed in bfloat16 or wider, within the bound.
A program may use at most 128 MiB of HBM per device.

v0:
```python
import functools

import jax
import jax.numpy as jnp
import numpy as np
from jax import lax
from jax.experimental import pallas as pl
from jax.experimental.pallas import tpu as pltpu
from jax.sharding import PartitionSpec as P

GROUPS = 32
SIDE = 8
RZ = 4
RY = 4
RX = 4
VOL = SIDE**3
SQ = SIDE * SIDE
NPOS = 16
UNROLL = 8
LANES = 2 * SQ
CHUNKS = VOL // LANES
norm_eps = 1e-05
MESH = pl.DeviceIdType.MESH
BF = jnp.bfloat16
F32 = jnp.float32
VM = pl.BlockSpec(memory_space=pltpu.VMEM)
SM = pl.BlockSpec(memory_space=pltpu.SMEM)


def constants(chans):
    v = np.arange(VOL)
    x, y, z = v % SIDE, v // SIDE % SIDE, v // SQ
    last = SIDE - 1
    lane = np.arange(LANES)
    near = [x < last, x > 0, y < last, y > 0]
    masks = [m[:LANES] for m in near] + [lane < SQ]
    masks += [lane // SIDE % SIDE == k for k in range(SIDE)]
    masks = np.broadcast_to(np.stack(masks)[:, None, :], (5 + SIDE, chans, LANES))
    half = SIDE // 2
    octant = z // half * 4 + y // half * 2 + x // half
    pool = (octant[None, :] == np.arange(8)[:, None]) / float(half**3)
    lanes = np.arange(8 * chans)
    spread = (np.arange(chans)[:, None] == lanes[None, :] % chans).astype(np.float32)
    octs = (lanes[:, None] // chans == octant[None, :]).astype(np.float32)
    as_bf = lambda a: jnp.asarray(np.asarray(a, np.float32), BF)
    return as_bf(masks), as_bf(pool), as_bf(spread), as_bf(octs)


def silu(x):
    h = 0.5 * x
    return h * jnp.tanh(h) + h


def face_slot(slot_at, face, k):
    a, b = k // 4, k % 4
    if face == 0:
        p = (a * RY + 0) * RX + b
    elif face == 1:
        p = (a * RY + RY - 1) * RX + b
    elif face == 2:
        p = (0 * RY + a) * RX + b
    else:
        p = ((RZ - 1) * RY + a) * RX + b
    return slot_at[p]


def chunk(ref, row, i):
    return ref[row, :, i * LANES : (i + 1) * LANES]


def turn(value, shift):
    return pltpu.roll(value, shift % LANES, 1) if shift % LANES else value


def side_tap(src, j, row, shift, span, keep):
    parts = []
    for i in range(CHUNKS):
        own = turn(chunk(src, j, i), -shift)
        near = turn(chunk(src, row, i), shift * (span - 1))
        parts.append(jnp.where(keep, own, near))
    return jnp.concatenate(parts, axis=1)


def depth_taps(src, j, up, down, low):
    turned = [turn(chunk(src, down, CHUNKS - 1), SQ)]
    turned += [turn(chunk(src, j, i), SQ) for i in range(CHUNKS)]
    turned += [turn(chunk(src, up, 0), SQ)]
    plus = [jnp.where(low, turned[i + 1], turned[i + 2]) for i in range(CHUNKS)]
    minus = [jnp.where(low, turned[i], turned[i + 1]) for i in range(CHUNKS)]
    return jnp.concatenate(plus, axis=1), jnp.concatenate(minus, axis=1)


def level_kernel(
    slots, chans, cells,
    slot_at, coords, counts, neighbours,
    feat, fine_w, gain, bias, pool, spread, masks,
    octs_h, down_h, up_h, weight_h,
    out, coarse_out,
    octs, down, up, weight,
    ext, ext2, acc, level, faces, halo, pooled, rows, coarse, stats,
    window, everyone, pad, part, result, lifted, nb, tgt,
    load, fsend, frecv, ssend, srecv, wsend, wrecv, rsend, rrecv,
):
    n_mx, n_my = lax.axis_size("mx"), lax.axis_size("my")
    mx, my = lax.axis_index("mx"), lax.axis_index("my")
    n = n_mx * n_my
    me = mx * n_my + my
    width = 8 * chans
    wide_c = gain.shape[1]

    loads = [
        pltpu.make_async_copy(a, b, load.at[i])
        for i, (a, b) in enumerate(
            ((down_h, down), (weight_h, weight),
             (up_h, up), (octs_h, octs))
        )
    ]
    for c in loads:
        c.start()

    barrier = pltpu.get_barrier_semaphore()

    def where_is(d):
        t = lax.rem(me + d, n)
        return (t // n_my, lax.rem(t, n_my))

    def greet(d, c):
        pl.semaphore_signal(barrier, inc=1, device_id=where_is(d), device_id_type=MESH)
        return c

    lax.fori_loop(1, n, greet, 0)

    ext[slots] = jnp.zeros((chans, VOL), BF)
    ext2[slots] = jnp.zeros((chans, VOL), BF)
    first_slot = me * slots
    count = counts[0]

    def tables(j):
        z = coords[0, j] - mx * RZ
        y = coords[1, j] - my * RY
        x = coords[2, j]
        for d in range(6):
            g = neighbours[d, j]
            here = g - first_slot
            spot = jnp.clip((z if d < 4 else y) * RX + x, 0, NPOS - 1)
            far = slots + 1 + max(d - 2, 0) * NPOS + spot
            inside = (here >= 0) & (here < slots)
            nb[d, j] = jnp.where(g < 0, slots, jnp.where(inside, here, far))
        q = (z // 2 * 2 + x // 2) * 2 + y // 2
        p = z % 2 * 4 + y % 2 * 2 + x % 2
        tgt[j] = jnp.clip(jnp.where(j < count, p * cells + q, 0), 0, 8 * cells - 1)

    def begin(j, c):
        s = silu(feat[j].astype(F32)).astype(BF)
        ext[j] = s
        return c

    lax.fori_loop(0, slots, begin, 0, unroll=UNROLL)
    keep = [masks[i] > 0.5 for i in range(5)]
    low_half = keep[4]

    peers = (
        (my > 0, mx, my - 1),
        (my < n_my - 1, mx, my + 1),
        (mx > 0, mx - 1, my),
        (mx < n_mx - 1, mx + 1, my),
    )

    def face_copy(r, f):
        _, a, b = peers[f]
        return pltpu.make_async_remote_copy(
            src_ref=faces.at[r, f], dst_ref=halo.at[r, f], send_sem=fsend.at[r, f],
            recv_sem=frecv.at[r, f], device_id=(a, b), device_id_type=MESH,
        )

    def send_faces(r, src):
        for f in range(4):
            rows_of = [face_slot(slot_at, f, k) for k in range(NPOS)]
            if f < 2:
                for g in range(2):
                    for i in range(CHUNKS):
                        mixed = None
                        for k in range(SIDE):
                            v = chunk(src, rows_of[g * SIDE + k], i)
                            v = turn(v, SIDE * k - f * (SQ - SIDE))
                            mixed = v if k == 0 else jnp.where(masks[5 + k] > 0.5, v, mixed)
                        faces[r, f, g * CHUNKS + i] = mixed
            else:
                i = 0 if f == 2 else CHUNKS - 1
                for k in range(NPOS // 2):
                    a, b = chunk(src, rows_of[2 * k], i), chunk(src, rows_of[2 * k + 1], i)
                    if f == 2:
                        b = turn(b, SQ)
                    else:
                        a = turn(a, SQ)
                    faces[r, f, k] = jnp.where(low_half, a, b)
            if r == 0 and f == 0:
                pl.semaphore_wait(barrier, n - 1)

            @pl.when(peers[f][0])
            def _():
                face_copy(r, f).start()

            @pl.when(jnp.logical_not(peers[f ^ 1][0]))
            def _():
                halo[r, f] = jnp.zeros_like(halo[r, f])

    def take_faces(r, dst):
        for f in range(4):
            @pl.when(peers[f][0])
            def _():
                face_copy(r, f).wait_send()

            @pl.when(peers[f ^ 1][0])
            def _():
                face_copy(r, f).wait_recv()

            for k in range(NPOS):
                row = slots + 1 + f * NPOS + k
                if f < 2:
                    for i in range(CHUNKS):
                        v = halo[r, f, k // SIDE * CHUNKS + i]
                        v = turn(v, f * (SQ - SIDE) - SIDE * (k % SIDE))
                        dst[row, :, i * LANES : (i + 1) * LANES] = v
                else:
                    i = 0 if f == 2 else CHUNKS - 1
                    v = halo[r, f, k // 2]
                    if k % 2 != f - 2:
                        v = turn(v, SQ)
                    dst[row, :, i * LANES : (i + 1) * LANES] = v

    def conv(r, base, src, finish):
        w = fine_w[r]
        w_near, w_far = w[:, : 3 * chans], w[:, 3 * chans :]

        def near_pass(j, c):
            if r == 0:
                tables(j)
            taps = [
                src[j],
                side_tap(src, j, nb[0, j], 1, SIDE, keep[0]),
                side_tap(src, j, nb[1, j], -1, SIDE, keep[1]),
            ]
            acc[j] = base[j].astype(F32) + jnp.dot(
                w_near, jnp.concatenate(taps, axis=0), preferred_element_type=F32
            )
            return c

        lax.fori_loop(0, slots, near_pass, 0, unroll=UNROLL)
        take_faces(r, src)

        def far_pass(j, c):
            taps = [
                side_tap(src, j, nb[2, j], SIDE, SIDE, keep[2]),
                side_tap(src, j, nb[3, j], -SIDE, SIDE, keep[3]),
                *depth_taps(src, j, nb[4, j], nb[5, j], low_half),
            ]
            finish(
                j,
                acc[j] + jnp.dot(
                    w_far, jnp.concatenate(taps, axis=0), preferred_element_type=F32
                ),
            )
            return c

        lax.fori_loop(0, slots, far_pass, 0, unroll=UNROLL)

    send_faces(0, ext)

    pooled[slots] = jnp.zeros((8, chans), F32)
    pm = pool[...]

    def first_done(j, value):
        f = value.astype(BF)
        level[j] = f
        pooled[j] = lax.dot_general(pm, f, (((1,), (1,)), ((), ())), preferred_element_type=F32)

    conv(0, feat, ext, first_done)
    for p in range(8):
        for q in range(cells):
            z = q // 4 * 2 + p // 4
            x = q // 2 % 2 * 2 + p % 2
            y = q % 2 * 2 + p // 2 % 2
            i = p * cells + q
            rows[i * 8 : (i + 1) * 8, :] = pooled[slot_at[(z * RY + y) * RX + x]]
    wide = jnp.dot(rows[...].astype(BF), spread[...], preferred_element_type=F32)
    m = 8 * cells
    oct_row = lax.broadcasted_iota(jnp.int32, (m * 8, width), 0) % 8
    oct_lane = lax.broadcasted_iota(jnp.int32, (m * 8, width), 1) // chans
    wide = jnp.where(oct_row == oct_lane, wide, 0.0)
    flat = jnp.sum(wide.reshape(m, 8, width), axis=1).astype(BF)
    loads[0].wait()
    ci = jnp.zeros((cells, wide_c), F32)
    for p in range(8):
        ci = ci + jnp.dot(
            flat[p * cells : (p + 1) * cells],
            down[p * width : (p + 1) * width, :],
            preferred_element_type=F32,
        )
    layer = cells // 2
    coarse[0] = ci[:layer]
    coarse[1] = ci[layer:]
    stats[0:1, :] = jnp.sum(ci, axis=0, keepdims=True)
    stats[1:2, :] = jnp.sum(ci * ci, axis=0, keepdims=True)

    def stat_copy(d):
        return pltpu.make_async_remote_copy(
            src_ref=stats, dst_ref=everyone.at[me], send_sem=ssend.at[d], recv_sem=srecv.at[d],
            device_id=where_is(d), device_id_type=MESH,
        )

    def stat_go(d, c):
        stat_copy(d).start()
        return c

    def stat_wait(d, c):
        stat_copy(d).wait()
        return c

    def win_copy(kind, d):
        t = lax.rem(my + d, n_my)
        if kind == 0:
            src, dst, a = coarse, window.at[my, pl.ds(1, 2)], mx
        elif kind == 1:
            src, dst, a = coarse.at[pl.ds(0, 1)], window.at[my, pl.ds(3, 1)], mx - 1
        else:
            src, dst, a = coarse.at[pl.ds(1, 1)], window.at[my, pl.ds(0, 1)], mx + 1
        return pltpu.make_async_remote_copy(
            src_ref=src, dst_ref=dst, send_sem=wsend.at[kind, d], recv_sem=wrecv.at[kind, d],
            device_id=(a, t), device_id_type=MESH,
        )

    lax.fori_loop(1, n, stat_go, 0)
    low, high = mx > 0, mx < n_mx - 1
    for d in range(n_my):
        if d:
            win_copy(0, d).start()

        @pl.when(low)
        def _():
            win_copy(1, d).start()

        @pl.when(high)
        def _():
            win_copy(2, d).start()
    window[my, 1:3] = coarse[...]
    everyone[me] = stats[...]

    @pl.when(jnp.logical_not(low))
    def _():
        for j in range(n_my):
            window[j, 0] = jnp.zeros_like(window[j, 0])

    @pl.when(jnp.logical_not(high))
    def _():
        for j in range(n_my):
            window[j, 3] = jnp.zeros_like(window[j, 3])

    pad[...] = jnp.zeros_like(pad)
    group = wide_c // GROUPS
    same = (
        lax.broadcasted_iota(jnp.int32, (wide_c, wide_c), 0) // group
        == lax.broadcasted_iota(jnp.int32, (wide_c, wide_c), 1) // group
    ).astype(F32)
    for c in loads[1:]:
        c.wait()
    for d in range(n_my):
        if d:
            win_copy(0, d).wait()

        @pl.when(low)
        def _():
            win_copy(1, d).wait_send()
            win_copy(2, d).wait_recv()

        @pl.when(high)
        def _():
            win_copy(2, d).wait_send()
            win_copy(1, d).wait_recv()
    lax.fori_loop(1, n, stat_wait, 0)

    total = float(cells * group) * n
    sums = jnp.sum(everyone[...], axis=0)
    sums = jnp.concatenate([sums, jnp.zeros((6, wide_c), F32)], axis=0)
    sums = jnp.dot(sums, same, precision=lax.Precision.HIGHEST, preferred_element_type=F32) / total
    mean = sums[0:1]
    std = jnp.sqrt(sums[1:2] - mean * mean + norm_eps)
    g = gain[...]
    b = bias[...]
    for zw in range(4):
        for j in range(n_my):
            value = silu((window[j, zw] - mean) / std * g + b)
            if zw == 0:
                value = jnp.where(low, value, 0.0)
            if zw == 3:
                value = jnp.where(high, value, 0.0)
            for x in range(2):
                pad[1 + x, zw, 1 + 2 * j : 3 + 2 * j, :] = value[2 * x : 2 * x + 2]
    tall = 2 * n_my
    sums = jnp.zeros((4 * tall, part.shape[2]), F32)
    t = 0
    for dz in range(3):
        for dy in range(3):
            for dx in range(3):
                lhs = jnp.concatenate(
                    [pad[x + dx, z + dz, dy : dy + tall, :] for z in range(2) for x in range(2)],
                    axis=0,
                ).astype(BF)
                sums = sums + lax.dot_general(
                    lhs, weight[:, t * wide_c : (t + 1) * wide_c], (((1,), (1,)), ((), ())),
                    preferred_element_type=F32,
                )
                t += 1
    for j in range(n_my):
        for zx in range(4):
            part[j, 2 * zx : 2 * zx + 2, :] = sums[zx * tall + 2 * j : zx * tall + 2 * j + 2, :]
    copies = []
    for d in range(1, n_my):
        to = lax.rem(my + d, n_my)
        copies.append(
            pltpu.make_async_remote_copy(
                src_ref=part.at[to], dst_ref=result.at[my], send_sem=rsend.at[d],
                recv_sem=rrecv.at[d], device_id=(mx, to), device_id_type=MESH,
            )
        )
    for c in copies:
        c.start()
    result[my] = part[my]
    for c in copies:
        c.wait()

    whole = jnp.concatenate([result[j] for j in range(n_my)], axis=1)
    co = (whole + jnp.concatenate([coarse[0], coarse[1]], axis=0)).astype(BF)
    cof = co.astype(F32)
    for z in range(2):
        for y in range(2):
            q = z * 4 + y
            pair = jnp.concatenate([cof[q : q + 1], cof[q + 2 : q + 3]], axis=0)
            coarse_out[z, y] = pair.astype(BF)
    wide = jnp.dot(co, up[...], preferred_element_type=F32)
    for p in range(8):
        for q in range(cells):
            lifted[p * cells + q] = wide[q : q + 1, p * width : (p + 1) * width]
    pick = (
        lax.broadcasted_iota(jnp.int32, (chans, width), 0)
        == lax.broadcasted_iota(jnp.int32, (chans, width), 1) % chans
    )
    oc = octs[...]

    def join(j, c):
        row = jnp.where(pick, lifted[tgt[j]], 0.0)
        hi = row.astype(BF)
        lo = (row - hi.astype(F32)).astype(BF)
        both = jnp.dot(jnp.concatenate([hi, lo], axis=0), oc, preferred_element_type=F32)
        f = (level[j].astype(F32) + (both[:chans] + both[chans:])).astype(BF)
        level[j] = f
        ext[j] = silu(f.astype(F32)).astype(BF)
        return c

    lax.fori_loop(0, slots, join, 0, unroll=UNROLL)
    send_faces(1, ext)

    def second_done(j, value):
        f = value.astype(BF)
        level[j] = f
        ext2[j] = silu(f.astype(F32)).astype(BF)

    conv(1, level, ext, second_done)
    send_faces(2, ext2)

    def last_done(j, value):
        out[j] = value.astype(BF)

    conv(2, level, ext2, last_done)


def local(
    features, coords, counts, neighbours, fine_weights, down_weight, up_weight, norm_gain,
    norm_bias, coarse_weight,
):
    slots, chans, _ = features.shape
    n_mx, n_my = lax.axis_size("mx"), lax.axis_size("my")
    major, minor = lax.axis_index("mx"), lax.axis_index("my")
    cells = (RZ // 2) * (RY // 2) * (RX // 2)
    width = down_weight.shape[1]
    masks, pool, spread, octs = constants(chans)
    ids = jnp.arange(slots, dtype=jnp.int32)
    lin = ((coords[0] - major * RZ) * RY + coords[1] - minor * RY) * RX + coords[2]
    lin = jnp.where(ids < counts[0], lin, -1)
    hit = lin[None, :] == jnp.arange(RZ * RY * RX, dtype=jnp.int32)[:, None]
    slot_at = slots + jnp.sum(jnp.where(hit, ids - slots, 0), axis=1)
    n = n_mx * n_my
    sds = jax.ShapeDtypeStruct
    weight_t = coarse_weight.T
    held = [
        pltpu.VMEM(a.shape, a.dtype)
        for a in (octs, down_weight, up_weight, weight_t)
    ]
    ext = pltpu.VMEM((slots + 1 + 4 * NPOS, chans, VOL), BF)
    ext_small = pltpu.VMEM((slots, chans, VOL), BF)
    dma = pltpu.SemaphoreType.DMA
    scratch = held + [
        ext, ext,
        pltpu.VMEM((slots, chans, VOL), F32),
        ext_small,
        pltpu.VMEM((3, 4, NPOS // 2, chans, LANES), BF),
        pltpu.VMEM((3, 4, NPOS // 2, chans, LANES), BF),
        pltpu.VMEM((slots + 1, 8, chans), F32),
        pltpu.VMEM((8 * cells * 8, chans), F32),
        pltpu.VMEM((2, cells // 2, width), F32),
        pltpu.VMEM((2, width), F32),
        pltpu.VMEM((n_my, 4, cells // 2, width), F32),
        pltpu.VMEM((n, 2, width), F32),
        pltpu.VMEM((4, 4, -(-(2 * n_my + 2) // 8) * 8, width), F32),
        pltpu.VMEM((n_my, cells, coarse_weight.shape[1]), F32),
        pltpu.VMEM((n_my, cells, coarse_weight.shape[1]), F32),
        pltpu.VMEM((8 * cells, 1, 8 * chans), F32),
        pltpu.SMEM((6, slots), jnp.int32),
        pltpu.SMEM((slots,), jnp.int32),
        dma((4,)), dma((3, 4)), dma((3, 4)), dma((n,)), dma((n,)),
        dma((3, n_my)), dma((3, n_my)), dma((n_my,)), dma((n_my,)),
    ]
    fine, out = pl.pallas_call(
        functools.partial(level_kernel, slots, chans, cells),
        out_shape=(sds(features.shape, BF), sds((RZ // 2, RY // 2, RX // 2, width), BF)),
        in_specs=[SM] * 4 + [VM] * 7 + [pl.BlockSpec(memory_space=pl.ANY)] * 4,
        out_specs=(VM, VM),
        scratch_shapes=scratch,
        compiler_params=pltpu.CompilerParams(collective_id=0, has_side_effects=True),
    )(
        slot_at, coords, counts, neighbours, features, fine_weights, norm_gain[None, :],
        norm_bias[None, :], pool, spread, masks, octs, down_weight, up_weight, weight_t,
    )
    fine = jnp.where((ids < counts[0])[:, None, None], fine, jnp.zeros_like(fine))
    return fine, out


def solution(mesh):
    in_specs = (
        P(("mx", "my"), None, None),
        P(None, ("mx", "my")),
        P(("mx", "my")),
        P(None, ("mx", "my")),
        P(),
        P(),
        P(),
        P(),
        P(),
        P(None, "my"),
    )
    out_specs = (P(("mx", "my"), None, None), P("mx", "my", None, None))
    return jax.shard_map(local, mesh=mesh, in_specs=in_specs, out_specs=out_specs, check_vma=False)
```

profile of v0, /device:TPU:0, one launch (start us, length us, event | category | flops | bytes accessed | tf_op | source)
XLA Modules:
  0.0 51.9 jit_solution(8879522477527984864)
XLA Ops:
  1.3 0.0 copy-start
  1.3 0.7 %copy-done = s32[3,32]{1,0:T(4,128)S(1)} copy-done((s32[3,32]{1,0:T(4,128)S(1)}, s32[3,32]{1,0:T(4,128)}, u32[]{:S(2)}) %copy-start) | copy-done | bytes 408
  2.0 0.1 select_reduce_fusion
  2.1 0.5 broadcast_add_fusion.slot_at
  2.6 46.3 %shard_map.149 = (bf16[32,32,512]{2,1,0:T(8,128)(2,1)}, bf16[2,2,2,256]{3,2,1,0:T(2,128)(2,1)}) custom-call(s32[64]{0:T(128)} %broadcast_add_fusion.slot_at, s32[3,32]{1,0:T(4,128)} %coords.1, s32[1]{0:T(128)} %copy.17.counts, s32[6,32]{1,0:T(8,128)} %neighbours.1, bf16[32,32,512]{2,1,0:T(8,128)(2,1)} %feat.1, bf16[3,32,224]{2,1,0:T(8,128)(2,1)} %fine_w.1, ...), custom_call_target="tpu_custom_call" | custom-call | tf_op jit(solution)/shard_map/pallas_call | solution.py:523
  48.9 0.0 copy-start.1
  48.9 2.3 %broadcast_select_fusion = bf16[32,32,512]{2,1,0:T(8,128)(2,1)} fusion(bf16[32,32,512]{2,1,0:T(8,128)(2,1)} %get-tuple-element.4, pred[32]{0:T(512)(128)(4,1)S(1)} %iota_compare_fusion.1), kind=kLoop, calls=%fused_computation | loop fusion | flops 524288 | bytes 2097184 | tf_op jit(solution)/shard_map/jit(_where)/select_n | solution.py:534
  51.3 0.0 copy-done.1
  51.3 0.6 %copy.18 = bf16[2,2,2,256]{3,2,1,0:T(2,128)(2,1)} copy(bf16[2,2,2,256]{3,2,1,0:T(2,128)(2,1)S(1)} %copy-done.1) | data formatting | bytes 8192
  (3 shorter events, 0.0 us)
Async XLA Ops:
  1.3 0.7 %copy-start = (s32[3,32]{1,0:T(4,128)S(1)}, s32[3,32]{1,0:T(4,128)}, u32[]{:S(2)}) copy-start(s32[3,32]{1,0:T(4,128)} %coords.1) | copy-start | bytes 1156
  48.9 2.3 %copy-start.1 = (bf16[2,2,2,256]{3,2,1,0:T(2,128)(2,1)S(1)}, bf16[2,2,2,256]{3,2,1,0:T(2,128)(2,1)}, u32[]{:S(2)}) copy-start(bf16[2,2,2,256]{3,2,1,0:T(2,128)(2,1)} %get-tuple-element.9) | copy-start | bytes 12292
where the time goes:
time: 52.1 us; the launch traced here: 51.9 us
  Pallas kernels  46.3 us (89%)
  other arithmetic  2.96 us (6%)
  between operations  1.31 us (3%)
  local copies, waits for them, and re-layouts  1.27 us (2%)
    pallas_call x1, Pallas kernels, local(): pl.pallas_call(functools.partial(level_kernel, slots, chans, cells), out_...  46.3 us
    select_n x1, other arithmetic, local(): jnp.where((ids < counts[0])[:, None, None], fine, jnp.zeros_like(fine))  2.34 us
    unnamed x5, local copies, waits for them, and re-layouts  1.27 us

commit v1 on v0

v1 whole, which is shorter than its diff:
```python
import functools

import jax
import jax.numpy as jnp
import numpy as np
from jax import lax
from jax.experimental import pallas as pl
from jax.experimental.pallas import tpu as pltpu
from jax.sharding import PartitionSpec as P

GROUPS = 32
SIDE = 8
RZ = 4
RY = 4
RX = 4
HALF = SIDE // 2
CUBES = HALF**3
PLANE = HALF**2
FACE = 16
norm_eps = 1e-05
MESH = pl.DeviceIdType.MESH
BF = jnp.bfloat16
F32 = jnp.float32
I32 = jnp.int32
VM = pl.BlockSpec(memory_space=pltpu.VMEM)
SM = pl.BlockSpec(memory_space=pltpu.SMEM)
NN = (((1,), (0,)), ((), ()))
NT = (((1,), (1,)), ((), ()))
TN = (((0,), (0,)), ((), ()))


def constants(chans):
    lane = np.arange(4 * chans)
    masks = np.stack([lane < 2 * chans, lane // chans % 2 == 0])
    masks = np.broadcast_to(masks[:, None, :], (2, 32, 4 * chans))
    sel = np.zeros((256, 256))
    for w in range(8):
        vy, vz, vx = w >> 2, w >> 1 & 1, w & 1
        for i in range(32):
            z, y, x = i // 16 * 2 + vz, i // 4 % 4 * 2 + vy, i % 4 * 2 + vx
            sel[w * 32 + i, (z * SIDE + y) * SIDE + x] = 1
    swap = np.zeros((256, 256))
    for i in range(16):
        for s in range(16):
            swap[i * 16 + s, s * 16 + i] = 1
    wide = np.arange(8 * chans)
    same = wide[:, None] % chans == wide[None, :] % chans
    as_bf = lambda a: jnp.asarray(np.asarray(a, np.float32), BF)
    return as_bf(masks), as_bf(sel), as_bf(swap), as_bf(same)


def dot(a, b, dims=NN):
    return lax.dot_general(a, b, dims, preferred_element_type=F32)


def silu(x):
    h = 0.5 * x
    return h * jnp.tanh(h) + h


def swap_blocks(parts, low64, low32):
    left, right = [p[0] for p in parts], [p[1] for p in parts]
    m = [(left[i], left[i + 4]) for i in range(4)] + [(right[i], right[i + 4]) for i in range(4)]
    for bit, low, up, down in ((2, low64, 64, 64), (1, low32, 32, 96)):
        n = list(m)
        for j in range(8):
            if j & bit:
                continue
            a, b = m[j], m[j | bit]
            n[j] = tuple(jnp.where(low, a[t], pltpu.roll(b[t], up, 1)) for t in range(2))
            n[j | bit] = tuple(jnp.where(low, pltpu.roll(a[t], down, 1), b[t]) for t in range(2))
        m = n
    return m


def level_kernel(
    slots, chans, cells,
    counts, coords, neighbours,
    feat, fine_w, gain, bias, sel, swap, same, masks,
    down_h, up_h, weight_h,
    fine, coarse_out,
    down, up, weight,
    blocks, base, sig, sig2, acc, wts, gx, gyp, gym, gz, faces, halo, term,
    coarse, stats, window, everyone, pad, part, result,
    load, fsend, frecv, ssend, srecv, wsend, wrecv, rsend, rrecv,
):
    n_mx, n_my = lax.axis_size("mx"), lax.axis_size("my")
    mx, my = lax.axis_index("mx"), lax.axis_index("my")
    n = n_mx * n_my
    me = mx * n_my + my
    width = 8 * chans
    side = width // 2
    wide_c = gain.shape[1]

    loads = [
        pltpu.make_async_copy(a, b, load.at[i])
        for i, (a, b) in enumerate(((down_h, down), (weight_h, weight), (up_h, up)))
    ]
    for c in loads:
        c.start()

    barrier = pltpu.get_barrier_semaphore()

    def where_is(d):
        t = lax.rem(me + d, n)
        return (t // n_my, lax.rem(t, n_my))

    def greet(d, c):
        pl.semaphore_signal(barrier, inc=1, device_id=where_is(d), device_id_type=MESH)
        return c

    lax.fori_loop(1, n, greet, 0)

    def rows(ref, q):
        return ref[q * slots : (q + 1) * slots, :]

    def left(ref, q):
        return ref[q * slots : (q + 1) * slots, :side]

    def right(ref, q):
        return ref[q * slots : (q + 1) * slots, side:]

    low64, low32 = masks[0] > 0.5, masks[1] > 0.5
    zero = jnp.zeros((slots, side), BF)

    for g in range(slots // 8):
        for h in range(2):
            x = feat[8 * g : 8 * g + 8, :, 256 * h : 256 * h + 256].reshape(8 * chans, 256)
            r = dot(sel[...], x, NT).astype(BF)
            m = [(r[32 * w : 32 * w + 32, :side], r[32 * w : 32 * w + 32, side:]) for w in range(8)]
            m = swap_blocks(m, low64, low32)
            for s in range(8):
                at = (8 * g + s) * CUBES + 32 * h
                blocks[at : at + 32, :side] = m[s][0]
                blocks[at : at + 32, side:] = m[s][1]
    for z in range(HALF):
        for g in range(slots // 16):
            x = jnp.concatenate(
                [blocks[(16 * g + s) * CUBES + 16 * z : (16 * g + s) * CUBES + 16 * z + 16, :]
                 for s in range(16)], axis=0)
            r = dot(swap[...], x)
            rb = r.astype(BF)
            rs = silu(r).astype(BF)
            for i in range(16):
                at = (16 * z + i) * slots + 16 * g
                base[at : at + 16, :] = rb[16 * i : 16 * i + 16]
                sig[at : at + 16, :] = rs[16 * i : 16 * i + 16]

    def one_hot(row, count):
        return (lax.broadcasted_iota(I32, (count, slots), 0) == row).astype(F32).astype(BF)

    eye = (
        lax.broadcasted_iota(I32, (slots, slots), 0) == lax.broadcasted_iota(I32, (slots, slots), 1)
    ).astype(F32).astype(BF)

    def turned(table):
        return dot(eye, table, NT).astype(BF)

    pz = coords[0:1, :] - mx * RZ
    py = coords[1:2, :] - my * RY
    px = coords[2:3, :]
    live = lax.broadcasted_iota(I32, (1, slots), 1) < counts[0]

    def link(d):
        g = neighbours[d : d + 1, :]
        here = g - me * slots
        inside = (here >= 0) & (here < slots)
        far = slots + (pz if d < 4 else py) * RX + px
        return jnp.where(g < 0, -1, jnp.where(inside, here, far))

    halo_rows = slots + FACE
    g_x = turned(jnp.concatenate([one_hot(link(d), slots) for d in (0, 1)], axis=0))
    g_yp = turned(one_hot(link(2), halo_rows))
    g_ym = turned(one_hot(link(3), halo_rows))
    g_z = turned(jnp.concatenate([one_hot(link(d), halo_rows) for d in (4, 5)], axis=0))
    edge = (
        jnp.where(live & (py == 0), pz * RX + px, -1),
        jnp.where(live & (py == RY - 1), pz * RX + px, -1),
        jnp.where(live & (pz == 0), py * RX + px, -1),
        jnp.where(live & (pz == RZ - 1), py * RX + px, -1),
    )
    g_edge = [one_hot(e, FACE) for e in edge]
    cell = (pz // 2 * 2 + px // 2) * 2 + py // 2
    place = pz % 2 * 4 + py % 2 * 2 + px % 2
    g_cell = one_hot(jnp.where(live, place * cells + cell, -1), 8 * cells)
    g_lift = turned(g_cell)
    alive = dot(
        jnp.where(live, eye.astype(F32), 0.0).astype(BF), jnp.ones((slots, width), BF)
    ) > 0.5

    peers = (
        (my > 0, mx, my - 1),
        (my < n_my - 1, mx, my + 1),
        (mx > 0, mx - 1, my),
        (mx < n_mx - 1, mx + 1, my),
    )

    def face_copy(r, f):
        _, a, b = peers[f]
        return pltpu.make_async_remote_copy(
            src_ref=faces.at[r, f], dst_ref=halo.at[r, f], send_sem=fsend.at[r, f],
            recv_sem=frecv.at[r, f], device_id=(a, b), device_id_type=MESH,
        )

    low64_face = low64[:FACE]

    def send_face(r, src, f):
        for k in range(PLANE // 2):
            a, x = k // 2, k % 2 * 2
            if f < 2:
                part_of = left if f == 0 else right
                q = a * PLANE + (0 if f == 0 else HALF - 1) * HALF + x
                pair = jnp.concatenate([part_of(src, q), part_of(src, q + 1)], axis=1)
                v = dot(g_edge[f], pair).astype(BF)
                faces[r, f, 2 * k] = v[:, :side]
                faces[r, f, 2 * k + 1] = v[:, side:]
            else:
                q = (0 if f == 2 else HALF - 1) * PLANE + a * HALF + x
                va = dot(g_edge[f], rows(src, q)).astype(BF)
                vb = dot(g_edge[f], rows(src, q + 1)).astype(BF)
                for t in range(2):
                    own = va[:, t * side : (t + 1) * side]
                    other = pltpu.roll(vb[:, t * side : (t + 1) * side], 64, 1)
                    if f == 2:
                        faces[r, f, 2 * k + t] = jnp.where(low64_face, own, other)
                    else:
                        faces[r, f, 2 * k + t] = jnp.where(low64_face, other, own)

        @pl.when(peers[f][0])
        def _():
            face_copy(r, f).start()

        @pl.when(jnp.logical_not(peers[f ^ 1][0]))
        def _():
            halo[r, f] = jnp.zeros_like(halo[r, f])

    def take_face(r, f):
        @pl.when(peers[f][0])
        def _():
            face_copy(r, f).wait_send()

        @pl.when(peers[f ^ 1][0])
        def _():
            face_copy(r, f).wait_recv()

    def z_halo(r, f, y, x):
        k = 2 * (y * 2 + x // 2)
        v = [halo[r, f, k + t] for t in range(2)]
        if x % 2:
            v = [pltpu.roll(a, 64, 1) for a in v]
        none = jnp.zeros_like(v[0])
        if f == 2:
            v = [jnp.where(low64_face, a, none) for a in v]
        else:
            v = [jnp.where(low64_face, none, a) for a in v]
        return jnp.concatenate(v, axis=1)

    def both(low, a, b):
        return jnp.concatenate([jnp.where(low, a[t], b[t]) for t in range(2)], axis=1)

    def halves(ref, q):
        return left(ref, q), right(ref, q)

    block = 8

    def near(r, src):
        for zy in range(PLANE):
            first, last = halves(src, zy * HALF), halves(src, zy * HALF + HALF - 1)
            pair = jnp.concatenate(
                [both(low32, first, (zero, zero)), both(low32, (zero, zero), last)], axis=0
            )
            gx[zy * slots : (zy + 1) * slots, :] = dot(g_x, pair).astype(BF)
        for b in range(CUBES // block):
            taps = []
            for q in range(b * block, (b + 1) * block):
                edge_of = halves(gx, q // HALF)
                after = halves(src, q + 1) if q % HALF < HALF - 1 else edge_of
                before = halves(src, q - 1) if q % HALF > 0 else edge_of
                taps.append(both(low32, after, before))
            span = slice(b * block * slots, (b + 1) * block * slots)
            acc[span, :] = base[span, :].astype(F32) + (
                dot(src[span, :], wts[r, 0]) + dot(jnp.concatenate(taps, axis=0), wts[r, 1])
            )

    def far(r, src, finish):
        for f in range(4):
            take_face(r, f)
        for k in range(PLANE // 2):
            z, x = k // 2, k % 2 * 2
            for f, part_of, table, out in ((0, left, g_yp, gyp), (1, right, g_ym, gym)):
                q = z * PLANE + (0 if f == 0 else HALF - 1) * HALF + x
                own = jnp.concatenate([part_of(src, q), part_of(src, q + 1)], axis=1)
                got = jnp.concatenate([halo[r, f, 2 * k], halo[r, f, 2 * k + 1]], axis=1)
                v = dot(table, jnp.concatenate([own, got], axis=0)).astype(BF)
                out[2 * k * slots : (2 * k + 1) * slots, :] = v[:, :side]
                out[(2 * k + 1) * slots : (2 * k + 2) * slots, :] = v[:, side:]
        for y in range(HALF):
            for x in range(HALF):
                i = y * HALF + x
                first, last = halves(src, i), halves(src, (HALF - 1) * PLANE + i)
                stack = jnp.concatenate(
                    [both(low64, first, (zero, zero)), z_halo(r, 2, y, x),
                     both(low64, (zero, zero), last), z_halo(r, 3, y, x)], axis=0,
                )
                gz[i * slots : (i + 1) * slots, :] = dot(g_z, stack).astype(BF)
        for b in range(CUBES // block):
            y_taps, z_taps = [], []
            for q in range(b * block, (b + 1) * block):
                z, y, x = q // PLANE, q // HALF % HALF, q % HALF
                zx = z * HALF + x
                span = slice(zx * slots, (zx + 1) * slots)
                after = left(src, q + HALF) if y < HALF - 1 else gyp[span, :]
                before = right(src, q - HALF) if y > 0 else gym[span, :]
                y_taps.append(jnp.concatenate([after, before], axis=1))
                edge_of = halves(gz, y * HALF + x)
                after = halves(src, q + PLANE) if z < HALF - 1 else edge_of
                before = halves(src, q - PLANE) if z > 0 else edge_of
                z_taps.append(both(low64, after, before))
            span = slice(b * block * slots, (b + 1) * block * slots)
            finish(span, acc[span, :] + (
                dot(jnp.concatenate(y_taps, axis=0), wts[r, 2])
                + dot(jnp.concatenate(z_taps, axis=0), wts[r, 3])
            ))

    lane_block = lax.broadcasted_iota(I32, (slots, width), 1) // chans
    block_f = lane_block.astype(F32).astype(BF)
    spread = (
        lax.broadcasted_iota(I32, (chans, width), 0)
        == lax.broadcasted_iota(I32, (chans, width), 1) % chans
    ).astype(F32).astype(BF)
    none = jnp.zeros((chans, width), BF)
    is_block = [block_f == float(w) for w in range(8)]

    def fill(r):
        t = dot(fine_w[r], spread, TN).astype(BF)
        t = [t[i * chans : (i + 1) * chans] for i in range(7)]
        for w in range(8):
            span = slice(w * chans, (w + 1) * chans)
            vy, vz, vx = w >> 2, w >> 1 & 1, w & 1
            v = jnp.where(is_block[w], t[0], none)
            v = jnp.where(is_block[w ^ 1], t[1] if vx else t[2], v)
            v = jnp.where(is_block[w ^ 4], t[3] if vy else t[4], v)
            v = jnp.where(is_block[w ^ 2], t[5] if vz else t[6], v)
            wts[r, 0, span, :] = v
            wts[r, 1, span, :] = jnp.where(is_block[w ^ 1], t[2] if vx else t[1], none)
            wts[r, 2, span, :] = jnp.where(is_block[w ^ 4], t[4] if vy else t[3], none)
            wts[r, 3, span, :] = jnp.where(is_block[w ^ 2], t[6] if vz else t[5], none)

    pl.semaphore_wait(barrier, n - 1)
    for f in range(4):
        send_face(0, sig, f)
    for r in range(3):
        fill(r)
    near(0, sig)

    def first_done(span, value):
        base[span, :] = value.astype(BF)

    far(0, sig, first_done)

    sums = []
    for o in range(8):
        total = None
        for i in range(8):
            z, y, x = (o >> 2) * 2 + (i >> 2), (o >> 1 & 1) * 2 + (i >> 1 & 1), (o & 1) * 2 + (i & 1)
            v = rows(base, (z * HALF + y) * HALF + x).astype(F32)
            total = v if i == 0 else total + v
        hi = total.astype(BF)
        sums += [hi, (total - hi.astype(F32)).astype(BF)]
    sums = dot(jnp.concatenate(sums, axis=0), same[...])
    pooled = jnp.zeros((slots, width), F32)
    for o in range(8):
        v = sums[2 * o * slots : (2 * o + 1) * slots] + sums[(2 * o + 1) * slots : (2 * o + 2) * slots]
        pooled = jnp.where(lane_block == o, v, pooled)
    pooled = (pooled * (1.0 / HALF**3)).astype(BF)
    flat = dot(g_cell, pooled).astype(BF)
    loads[0].wait()
    ci = jnp.zeros((cells, wide_c), F32)
    for p in range(8):
        ci = ci + jnp.dot(
            flat[p * cells : (p + 1) * cells],
            down[p * width : (p + 1) * width, :],
            preferred_element_type=F32,
        )
    layer = cells // 2
    coarse[0] = ci[:layer]
    coarse[1] = ci[layer:]
    stats[0:1, :] = jnp.sum(ci, axis=0, keepdims=True)
    stats[1:2, :] = jnp.sum(ci * ci, axis=0, keepdims=True)

    def stat_copy(d):
        return pltpu.make_async_remote_copy(
            src_ref=stats, dst_ref=everyone.at[me], send_sem=ssend.at[d], recv_sem=srecv.at[d],
            device_id=where_is(d), device_id_type=MESH,
        )

    def stat_go(d, c):
        stat_copy(d).start()
        return c

    def stat_wait(d, c):
        stat_copy(d).wait()
        return c

    def win_copy(kind, d):
        t = lax.rem(my + d, n_my)
        if kind == 0:
            src, dst, a = coarse, window.at[my, pl.ds(1, 2)], mx
        elif kind == 1:
            src, dst, a = coarse.at[pl.ds(0, 1)], window.at[my, pl.ds(3, 1)], mx - 1
        else:
            src, dst, a = coarse.at[pl.ds(1, 1)], window.at[my, pl.ds(0, 1)], mx + 1
        return pltpu.make_async_remote_copy(
            src_ref=src, dst_ref=dst, send_sem=wsend.at[kind, d], recv_sem=wrecv.at[kind, d],
            device_id=(a, t), device_id_type=MESH,
        )

    lax.fori_loop(1, n, stat_go, 0)
    low, high = mx > 0, mx < n_mx - 1
    for d in range(n_my):
        if d:
            win_copy(0, d).start()

        @pl.when(low)
        def _():
            win_copy(1, d).start()

        @pl.when(high)
        def _():
            win_copy(2, d).start()
    window[my, 1:3] = coarse[...]
    everyone[me] = stats[...]

    @pl.when(jnp.logical_not(low))
    def _():
        for j in range(n_my):
            window[j, 0] = jnp.zeros_like(window[j, 0])

    @pl.when(jnp.logical_not(high))
    def _():
        for j in range(n_my):
            window[j, 3] = jnp.zeros_like(window[j, 3])

    pad[...] = jnp.zeros_like(pad)
    group = wide_c // GROUPS
    pooling = (
        lax.broadcasted_iota(jnp.int32, (wide_c, wide_c), 0) // group
        == lax.broadcasted_iota(jnp.int32, (wide_c, wide_c), 1) // group
    ).astype(F32)
    for c in loads[1:]:
        c.wait()
    for d in range(n_my):
        if d:
            win_copy(0, d).wait()

        @pl.when(low)
        def _():
            win_copy(1, d).wait_send()
            win_copy(2, d).wait_recv()

        @pl.when(high)
        def _():
            win_copy(2, d).wait_send()
            win_copy(1, d).wait_recv()
    lax.fori_loop(1, n, stat_wait, 0)

    total = float(cells * group) * n
    sums = jnp.sum(everyone[...], axis=0)
    sums = jnp.concatenate([sums, jnp.zeros((6, wide_c), F32)], axis=0)
    sums = jnp.dot(sums, pooling, precision=lax.Precision.HIGHEST, preferred_element_type=F32) / total
    mean = sums[0:1]
    std = jnp.sqrt(sums[1:2] - mean * mean + norm_eps)
    g = gain[...]
    b = bias[...]
    for zw in range(4):
        for j in range(n_my):
            value = silu((window[j, zw] - mean) / std * g + b)
            if zw == 0:
                value = jnp.where(low, value, 0.0)
            if zw == 3:
                value = jnp.where(high, value, 0.0)
            for x in range(2):
                pad[1 + x, zw, 1 + 2 * j : 3 + 2 * j, :] = value[2 * x : 2 * x + 2]
    tall = 2 * n_my
    sums = jnp.zeros((4 * tall, part.shape[2]), F32)
    t = 0
    for dz in range(3):
        for dy in range(3):
            for dx in range(3):
                lhs = jnp.concatenate(
                    [pad[x + dx, z + dz, dy : dy + tall, :] for z in range(2) for x in range(2)],
                    axis=0,
                ).astype(BF)
                sums = sums + lax.dot_general(
                    lhs, weight[:, t * wide_c : (t + 1) * wide_c], (((1,), (1,)), ((), ())),
                    preferred_element_type=F32,
                )
                t += 1
    for j in range(n_my):
        for zx in range(4):
            part[j, 2 * zx : 2 * zx + 2, :] = sums[zx * tall + 2 * j : zx * tall + 2 * j + 2, :]
    copies = []
    for d in range(1, n_my):
        to = lax.rem(my + d, n_my)
        copies.append(
            pltpu.make_async_remote_copy(
                src_ref=part.at[to], dst_ref=result.at[my], send_sem=rsend.at[d],
                recv_sem=rrecv.at[d], device_id=(mx, to), device_id_type=MESH,
            )
        )
    for c in copies:
        c.start()
    result[my] = part[my]
    for c in copies:
        c.wait()

    whole = jnp.concatenate([result[j] for j in range(n_my)], axis=1)
    co = (whole + jnp.concatenate([coarse[0], coarse[1]], axis=0)).astype(BF)
    cof = co.astype(F32)
    for z in range(2):
        for y in range(2):
            q = z * 4 + y
            pair = jnp.concatenate([cof[q : q + 1], cof[q + 2 : q + 3]], axis=0)
            coarse_out[z, y] = pair.astype(BF)
    wide = jnp.dot(co, up[...], preferred_element_type=F32)
    lifted = jnp.concatenate([wide[:, p * width : (p + 1) * width] for p in range(8)], axis=0)
    hi = lifted.astype(BF)
    lo = (lifted - hi.astype(F32)).astype(BF)
    picked = [dot(g_lift, v).astype(BF) for v in (hi, lo)]
    spots = [jnp.where(is_block[o], v, jnp.zeros_like(v)) for o in range(8) for v in picked]
    sums = dot(jnp.concatenate(spots, axis=0), same[...])
    for o in range(8):
        v = sums[2 * o * slots : (2 * o + 1) * slots] + sums[(2 * o + 1) * slots : (2 * o + 2) * slots]
        term[o * slots : (o + 1) * slots, :] = v

    for q in range(CUBES):
        z, y, x = q // PLANE, q // HALF % HALF, q % HALF
        o = z // 2 * 4 + y // 2 * 2 + x // 2
        span = slice(q * slots, (q + 1) * slots)
        f = (base[span, :].astype(F32) + term[o * slots : (o + 1) * slots, :]).astype(BF)
        base[span, :] = f
        sig[span, :] = silu(f.astype(F32)).astype(BF)
    for f in range(4):
        send_face(1, sig, f)

    def second_done(span, value):
        f = value.astype(BF)
        base[span, :] = f
        sig2[span, :] = silu(f.astype(F32)).astype(BF)

    near(1, sig)
    far(1, sig, second_done)
    for f in range(4):
        send_face(2, sig2, f)

    def last_done(span, value):
        for i in range(block):
            at = slice(i * slots, (i + 1) * slots)
            fine[span.start + at.start : span.start + at.stop, :] = jnp.where(
                alive, value[at], 0.0
            ).astype(BF)

    near(2, sig2)
    far(2, sig2, last_done)


def unfold_kernel(slots, chans, rows, coarse, sel, swap, masks, fine, coarse_out, blocks):
    width = 8 * chans
    side = width // 2
    low64, low32 = masks[0] > 0.5, masks[1] > 0.5
    for z in range(HALF):
        for g in range(slots // 16):
            x = jnp.concatenate(
                [rows[(16 * z + i) * slots + 16 * g : (16 * z + i) * slots + 16 * g + 16, :]
                 for i in range(16)], axis=0)
            r = dot(swap[...], x).astype(BF)
            for s in range(16):
                at = (16 * g + s) * CUBES + 16 * z
                blocks[at : at + 16, :] = r[16 * s : 16 * s + 16]
    for g in range(slots // 8):
        for h in range(2):
            m = []
            for s in range(8):
                at = (8 * g + s) * CUBES + 32 * h
                m.append((blocks[at : at + 32, :side], blocks[at : at + 32, side:]))
            m = swap_blocks(m, low64, low32)
            x = jnp.concatenate([jnp.concatenate(p, axis=1) for p in m], axis=0)
            r = dot(x.T, sel[...]).astype(BF)
            fine[8 * g : 8 * g + 8, :, 256 * h : 256 * h + 256] = r.reshape(8, chans, 256)
    coarse_out[...] = coarse[...]


def local(
    features, coords, counts, neighbours, fine_weights, down_weight, up_weight, norm_gain,
    norm_bias, coarse_weight,
):
    slots, chans, _ = features.shape
    n_mx, n_my = lax.axis_size("mx"), lax.axis_size("my")
    cells = (RZ // 2) * (RY // 2) * (RX // 2)
    width = down_weight.shape[1]
    lanes = 8 * chans
    masks, sel, swap, same = constants(chans)
    n = n_mx * n_my
    sds = jax.ShapeDtypeStruct
    weight_t = coarse_weight.T
    held = [pltpu.VMEM(a.shape, a.dtype) for a in (down_weight, up_weight, weight_t)]
    dma = pltpu.SemaphoreType.DMA
    total = slots * CUBES
    plane = slots * PLANE
    scratch = held + [
        pltpu.VMEM((total, lanes), BF),
        pltpu.VMEM((total, lanes), BF),
        pltpu.VMEM((total, lanes), BF),
        pltpu.VMEM((total, lanes), BF),
        pltpu.VMEM((total, lanes), F32),
        pltpu.VMEM((3, 4, lanes, lanes), BF),
        pltpu.VMEM((plane, lanes), BF),
        pltpu.VMEM((plane, lanes // 2), BF),
        pltpu.VMEM((plane, lanes // 2), BF),
        pltpu.VMEM((plane, lanes), BF),
        pltpu.VMEM((3, 4, PLANE, FACE, lanes // 2), BF),
        pltpu.VMEM((3, 4, PLANE, FACE, lanes // 2), BF),
        pltpu.VMEM((8 * slots, lanes), F32),
        pltpu.VMEM((2, cells // 2, width), F32),
        pltpu.VMEM((2, width), F32),
        pltpu.VMEM((n_my, 4, cells // 2, width), F32),
        pltpu.VMEM((n, 2, width), F32),
        pltpu.VMEM((4, 4, -(-(2 * n_my + 2) // 8) * 8, width), F32),
        pltpu.VMEM((n_my, cells, coarse_weight.shape[1]), F32),
        pltpu.VMEM((n_my, cells, coarse_weight.shape[1]), F32),
        dma((3,)), dma((3, 4)), dma((3, 4)), dma((n,)), dma((n,)),
        dma((3, n_my)), dma((3, n_my)), dma((n_my,)), dma((n_my,)),
    ]
    small = (RZ // 2, RY // 2, RX // 2, width)
    rows, coarse = pl.pallas_call(
        functools.partial(level_kernel, slots, chans, cells),
        out_shape=(sds((total, lanes), BF), sds(small, BF)),
        in_specs=[SM] + [VM] * 10 + [pl.BlockSpec(memory_space=pl.ANY)] * 3,
        out_specs=(VM, VM),
        scratch_shapes=scratch,
        compiler_params=pltpu.CompilerParams(collective_id=0, has_side_effects=True),
    )(
        counts, coords, neighbours, features, fine_weights, norm_gain[None, :],
        norm_bias[None, :], sel, swap, same, masks, down_weight, up_weight, weight_t,
    )
    return pl.pallas_call(
        functools.partial(unfold_kernel, slots, chans),
        out_shape=(sds(features.shape, BF), sds(small, BF)),
        in_specs=[VM] * 5,
        out_specs=(VM, VM),
        scratch_shapes=[pltpu.VMEM((total, lanes), BF)],
    )(rows, coarse, sel, swap, masks)


def solution(mesh):
    in_specs = (
        P(("mx", "my"), None, None),
        P(None, ("mx", "my")),
        P(("mx", "my")),
        P(None, ("mx", "my")),
        P(),
        P(),
        P(),
        P(),
        P(),
        P(None, "my"),
    )
    out_specs = (P(("mx", "my"), None, None), P("mx", "my", None, None))
    return jax.shard_map(local, mesh=mesh, in_specs=in_specs, out_specs=out_specs, check_vma=False)
```

time: 52.1 us -> 41.2 us (0.79)
  Pallas kernels: 46.3 us -> 39.7 us
  other arithmetic: 2.96 us -> 0 us
  local copies, waits for them, and re-layouts: 1.27 us -> 0 us
    pallas_call x1, Pallas kernels: 46.3 us -> 35.9 us  [local(): pl.pallas_call(functools.partial(level_kernel, slots, chans, cells), out_...]
    pallas_call x0 -> x1, Pallas kernels: none -> 3.85 us  [local(): pl.pallas_call(functools.partial(unfold_kernel, slots, chans), out_shape=...]
    select_n x1 -> x0, other arithmetic: 2.34 us -> none  [local(): jnp.where((ids < counts[0])[:, None, None], fine, jnp.zeros_like(fine))]
    unnamed x5 -> x0, local copies, waits for them, and re-layouts: 1.27 us -> none
where the time goes in v1:
time: 41.2 us; the launch traced here: 41 us
  Pallas kernels  39.7 us (96%)
  between operations  1.29 us (3%)
    pallas_call x1, Pallas kernels, local(): pl.pallas_call(functools.partial(level_kernel, slots, chans, cells), out_...  35.9 us
    pallas_call x1, Pallas kernels, local(): pl.pallas_call(functools.partial(unfold_kernel, slots, chans), out_shape=...  3.85 us

profile of v1, /device:TPU:0, one launch (start us, length us, event | category | flops | bytes accessed | tf_op | source)
XLA Modules:
  0.0 41.0 jit_solution(778282430914097332)
XLA Ops:
  1.3 35.9 %shard_map.149 = (bf16[2048,256]{1,0:T(8,128)(2,1)}, bf16[2,2,2,256]{3,2,1,0:T(2,128)(2,1)}) custom-call(s32[1]{0:T(128)S(6)} %copy.16.counts, s32[3,32]{1,0:T(4,128)} %coords.1, s32[6,32]{1,0:T(8,128)} %neighbours.1, bf16[32,32,512]{2,1,0:T(8,128)(2,1)} %feat.1, bf16[3,32,224]{2,1,0:T(8,128)(2,1)} %fine_w.1, f32[1,256]{1,0:T(1,128)} %bitcast.4, ...), custom_call_target="tpu_custom_call" | custom-call | tf_op jit(solution)/shard_map/pallas_call | solution.py:635
  37.1 3.8 %shard_map.150 = (bf16[32,32,512]{2,1,0:T(8,128)(2,1)}, bf16[2,2,2,256]{3,2,1,0:T(2,128)(2,1)}) custom-call(bf16[2048,256]{1,0:T(8,128)(2,1)} %get-tuple-element.4.rows, bf16[2,2,2,256]{3,2,1,0:T(2,128)(2,1)} %get-tuple-element.5.coarse, bf16[256,256]{1,0:T(8,128)(2,1)} %constant.9.clone.sel, bf16[256,256]{1,0:T(8,128)(2,1)} %constant.10.clone.swap, ...), custom_call_target="tpu_custom_call" | custom-call | tf_op jit(solution)/shard_map/pallas_call | solution.py:646

commit v2 on v1

--- a/solution.py
+++ b/solution.py
@@ -23,7 +23,7 @@
 F32 = jnp.float32
 I32 = jnp.int32
 VM = pl.BlockSpec(memory_space=pltpu.VMEM)
-SM = pl.BlockSpec(memory_space=pltpu.SMEM)
+HBM = pl.BlockSpec(memory_space=pl.ANY)
 NN = (((1,), (0,)), ((), ()))
 NT = (((1,), (1,)), ((), ()))
 TN = (((0,), (0,)), ((), ()))
@@ -75,14 +75,13 @@
 
 def level_kernel(
     slots, chans, cells,
-    counts, coords, neighbours,
-    feat, fine_w, gain, bias, sel, swap, same, masks,
-    down_h, up_h, weight_h,
+    counts_h, coords_h, neighbours_h, feat_h, fine_w_h, gain_h, bias_h, sel_h, swap_h, same_h,
+    masks_h, down_h, up_h, weight_h,
     fine, coarse_out,
-    down, up, weight,
+    counts, coords, neighbours, feat, fine_w, gain, bias, sel, swap, same, masks, down, up, weight,
     blocks, base, sig, sig2, acc, wts, gx, gyp, gym, gz, faces, halo, term,
     coarse, stats, window, everyone, pad, part, result,
-    load, fsend, frecv, ssend, srecv, wsend, wrecv, rsend, rrecv,
+    load, fsend, frecv, ssend, srecv, wsend, wrecv, rsend, rrecv, ready, store,
 ):
     n_mx, n_my = lax.axis_size("mx"), lax.axis_size("my")
     mx, my = lax.axis_index("mx"), lax.axis_index("my")
@@ -92,24 +91,69 @@
     side = width // 2
     wide_c = gain.shape[1]
 
-    loads = [
-        pltpu.make_async_copy(a, b, load.at[i])
-        for i, (a, b) in enumerate(((down_h, down), (weight_h, weight), (up_h, up)))
-    ]
-    for c in loads:
-        c.start()
+    order = (
+        ("feat", feat_h, feat), ("sel", sel_h, sel), ("masks", masks_h, masks),
+        ("swap", swap_h, swap), ("fine_w", fine_w_h, fine_w), ("counts", counts_h, counts),
+        ("coords", coords_h, coords), ("neighbours", neighbours_h, neighbours),
+        ("same", same_h, same), ("down", down_h, down), ("gain", gain_h, gain),
+        ("bias", bias_h, bias), ("weight", weight_h, weight), ("up", up_h, up),
+    )
+    loads = {
+        name: pltpu.make_async_copy(a, b, load.at[i]) for i, (name, a, b) in enumerate(order)
+    }
+    for name, _, _ in order:
+        loads[name].start()
 
     barrier = pltpu.get_barrier_semaphore()
+    low, high = mx > 0, mx < n_mx - 1
+
+    def greet(a, b):
+        pl.semaphore_signal(barrier, inc=1, device_id=(a, b), device_id_type=MESH)
+
+    @pl.when(low)
+    def _():
+        greet(mx - 1, my)
+
+    @pl.when(high)
+    def _():
+        greet(mx + 1, my)
+
+    for d in range(1, n_my):
+        greet(mx, lax.rem(my + d, n_my))
+
+    def entered():
+        pl.semaphore_wait(barrier, n_my - 1 + low.astype(I32) + high.astype(I32))
+
+    rounds = max(n_mx - 1, 0).bit_length()
+
+    def tell(k):
+        @pl.when(mx + 2**k < n_mx)
+        def _():
+            pl.semaphore_signal(
+                ready.at[k, 0], inc=1, device_id=(mx + 2**k, my), device_id_type=MESH
+            )
+
+        @pl.when(mx - 2**k >= 0)
+        def _():
+            pl.semaphore_signal(
+                ready.at[k, 1], inc=1, device_id=(mx - 2**k, my), device_id_type=MESH
+            )
+
+    def hear(k):
+        @pl.when(mx - 2**k >= 0)
+        def _():
+            pl.semaphore_wait(ready.at[k, 0], 1)
+
+        @pl.when(mx + 2**k < n_mx)
+        def _():
+            pl.semaphore_wait(ready.at[k, 1], 1)
 
     def where_is(d):
         t = lax.rem(me + d, n)
         return (t // n_my, lax.rem(t, n_my))
 
-    def greet(d, c):
-        pl.semaphore_signal(barrier, inc=1, device_id=where_is(d), device_id_type=MESH)
-        return c
-
-    lax.fori_loop(1, n, greet, 0)
+    for name in ("feat", "sel", "masks"):
+        loads[name].wait()
 
     def rows(ref, q):
         return ref[q * slots : (q + 1) * slots, :]
@@ -133,6 +177,7 @@
                 at = (8 * g + s) * CUBES + 32 * h
                 blocks[at : at + 32, :side] = m[s][0]
                 blocks[at : at + 32, side:] = m[s][1]
+    loads["swap"].wait()
     for z in range(HALF):
         for g in range(slots // 16):
             x = jnp.concatenate(
@@ -146,6 +191,8 @@
                 base[at : at + 16, :] = rb[16 * i : 16 * i + 16]
                 sig[at : at + 16, :] = rs[16 * i : 16 * i + 16]
 
+    for name in ("counts", "coords", "neighbours"):
+        loads[name].wait()
     def one_hot(row, count):
         return (lax.broadcasted_iota(I32, (count, slots), 0) == row).astype(F32).astype(BF)
 
@@ -159,7 +206,7 @@
     pz = coords[0:1, :] - mx * RZ
     py = coords[1:2, :] - my * RY
     px = coords[2:3, :]
-    live = lax.broadcasted_iota(I32, (1, slots), 1) < counts[0]
+    live = lax.broadcasted_iota(I32, (1, slots), 1) < counts[...]
 
     def link(d):
         g = neighbours[d : d + 1, :]
@@ -234,11 +281,13 @@
         def _():
             halo[r, f] = jnp.zeros_like(halo[r, f])
 
+    def sent_faces(r):
+        for f in range(4):
+            @pl.when(peers[f][0])
+            def _():
+                face_copy(r, f).wait_send()
+
     def take_face(r, f):
-        @pl.when(peers[f][0])
-        def _():
-            face_copy(r, f).wait_send()
-
         @pl.when(peers[f ^ 1][0])
         def _():
             face_copy(r, f).wait_recv()
@@ -261,66 +310,133 @@
     def halves(ref, q):
         return left(ref, q), right(ref, q)
 
-    block = 8
-
-    def near(r, src):
+    def run(ref, z, y):
+        at = (z * HALF + y) * HALF * slots
+        return ref[at : at + HALF * slots, :]
+
+    def spans(runs):
+        return [
+            slice((z * HALF + y) * HALF * slots, (z * HALF + y + 1) * HALF * slots)
+            for z, y in runs
+        ]
+
+    def stack(parts):
+        return jnp.concatenate(parts, axis=0)
+
+    def x_taps(src, runs):
+        taps = []
+        for z, y in runs:
+            edge_of = halves(gx, z * HALF + y)
+            for x in range(HALF):
+                q = (z * HALF + y) * HALF + x
+                after = halves(src, q + 1) if x < HALF - 1 else edge_of
+                before = halves(src, q - 1) if x > 0 else edge_of
+                taps.append(both(low32, after, before))
+        return stack(taps)
+
+    def y_taps(src, runs):
+        taps = []
+        for z, y in runs:
+            for x in range(HALF):
+                q = (z * HALF + y) * HALF + x
+                zx = z * HALF + x
+                span = slice(zx * slots, (zx + 1) * slots)
+                after = left(src, q + HALF) if y < HALF - 1 else gyp[span, :]
+                before = right(src, q - HALF) if y > 0 else gym[span, :]
+                taps.append(jnp.concatenate([after, before], axis=1))
+        return stack(taps)
+
+    def z_taps(src, runs):
+        taps = []
+        for z, y in runs:
+            for x in range(HALF):
+                q = (z * HALF + y) * HALF + x
+                edge_of = halves(gz, y * HALF + x)
+                after = halves(src, q + PLANE) if z < HALF - 1 else edge_of
+                before = halves(src, q - PLANE) if z > 0 else edge_of
+                taps.append(both(low64, after, before))
+        return stack(taps)
+
+    def passes(r, src, runs, kinds):
+        taps = {
+            0: lambda: stack([run(src, z, y) for z, y in runs]),
+            1: lambda: x_taps(src, runs),
+            2: lambda: y_taps(src, runs),
+            3: lambda: z_taps(src, runs),
+        }
+        total = None
+        for k in kinds:
+            v = dot(taps[k](), wts[r, k])
+            total = v if total is None else total + v
+        return total
+
+    def add_to(ref, runs, value):
+        tall = HALF * slots
+        return [
+            (span, ref[span, :].astype(F32) + value[i * tall : (i + 1) * tall])
+            for i, span in enumerate(spans(runs))
+        ]
+
+    inner, outer = range(1, HALF - 1), (0, HALF - 1)
+
+    def near(r, src, finish):
         for zy in range(PLANE):
             first, last = halves(src, zy * HALF), halves(src, zy * HALF + HALF - 1)
             pair = jnp.concatenate(
                 [both(low32, first, (zero, zero)), both(low32, (zero, zero), last)], axis=0
             )
             gx[zy * slots : (zy + 1) * slots, :] = dot(g_x, pair).astype(BF)
-        for b in range(CUBES // block):
-            taps = []
-            for q in range(b * block, (b + 1) * block):
-                edge_of = halves(gx, q // HALF)
-                after = halves(src, q + 1) if q % HALF < HALF - 1 else edge_of
-                before = halves(src, q - 1) if q % HALF > 0 else edge_of
-                taps.append(both(low32, after, before))
-            span = slice(b * block * slots, (b + 1) * block * slots)
-            acc[span, :] = base[span, :].astype(F32) + (
-                dot(src[span, :], wts[r, 0]) + dot(jnp.concatenate(taps, axis=0), wts[r, 1])
-            )
-
-    def far(r, src, finish):
-        for f in range(4):
+        for y in outer:
+            for zs, kinds in ((inner, (0, 1, 3)), (outer, (0, 1))):
+                runs = [(z, y) for z in zs]
+                for span, v in add_to(base, runs, passes(r, src, runs, kinds)):
+                    acc[span, :] = v
+        for z in outer:
+            runs = [(z, y) for y in inner]
+            for span, v in add_to(base, runs, passes(r, src, runs, (0, 1, 2))):
+                acc[span, :] = v
+        for z in inner:
+            runs = [(z, y) for y in inner]
+            for span, v in add_to(base, runs, passes(r, src, runs, (0, 1, 2, 3))):
+                finish(span, v)
+
+    def far_z(r, src, finish):
+        for f in (2, 3):
             take_face(r, f)
-        for k in range(PLANE // 2):
-            z, x = k // 2, k % 2 * 2
-            for f, part_of, table, out in ((0, left, g_yp, gyp), (1, right, g_ym, gym)):
-                q = z * PLANE + (0 if f == 0 else HALF - 1) * HALF + x
-                own = jnp.concatenate([part_of(src, q), part_of(src, q + 1)], axis=1)
-                got = jnp.concatenate([halo[r, f, 2 * k], halo[r, f, 2 * k + 1]], axis=1)
-                v = dot(table, jnp.concatenate([own, got], axis=0)).astype(BF)
-                out[2 * k * slots : (2 * k + 1) * slots, :] = v[:, :side]
-                out[(2 * k + 1) * slots : (2 * k + 2) * slots, :] = v[:, side:]
         for y in range(HALF):
             for x in range(HALF):
                 i = y * HALF + x
                 first, last = halves(src, i), halves(src, (HALF - 1) * PLANE + i)
-                stack = jnp.concatenate(
+                both_z = jnp.concatenate(
                     [both(low64, first, (zero, zero)), z_halo(r, 2, y, x),
                      both(low64, (zero, zero), last), z_halo(r, 3, y, x)], axis=0,
                 )
-                gz[i * slots : (i + 1) * slots, :] = dot(g_z, stack).astype(BF)
-        for b in range(CUBES // block):
-            y_taps, z_taps = [], []
-            for q in range(b * block, (b + 1) * block):
-                z, y, x = q // PLANE, q // HALF % HALF, q % HALF
-                zx = z * HALF + x
-                span = slice(zx * slots, (zx + 1) * slots)
-                after = left(src, q + HALF) if y < HALF - 1 else gyp[span, :]
-                before = right(src, q - HALF) if y > 0 else gym[span, :]
-                y_taps.append(jnp.concatenate([after, before], axis=1))
-                edge_of = halves(gz, y * HALF + x)
-                after = halves(src, q + PLANE) if z < HALF - 1 else edge_of
-                before = halves(src, q - PLANE) if z > 0 else edge_of
-                z_taps.append(both(low64, after, before))
-            span = slice(b * block * slots, (b + 1) * block * slots)
-            finish(span, acc[span, :] + (
-                dot(jnp.concatenate(y_taps, axis=0), wts[r, 2])
-                + dot(jnp.concatenate(z_taps, axis=0), wts[r, 3])
-            ))
+                gz[i * slots : (i + 1) * slots, :] = dot(g_z, both_z).astype(BF)
+        for z in outer:
+            runs = [(z, y) for y in inner]
+            for span, v in add_to(acc, runs, passes(r, src, runs, (3,))):
+                finish(span, v)
+        for y in outer:
+            runs = [(z, y) for z in outer]
+            for span, v in add_to(acc, runs, passes(r, src, runs, (3,))):
+                acc[span, :] = v
+
+    def far_y(r, src, finish, f):
+        take_face(r, f)
+        part_of, table, out = ((left, g_yp, gyp), (right, g_ym, gym))[f]
+        for k in range(PLANE // 2):
+            z, x = k // 2, k % 2 * 2
+            q = z * PLANE + (0 if f == 0 else HALF - 1) * HALF + x
+            own = jnp.concatenate([part_of(src, q), part_of(src, q + 1)], axis=1)
+            got = jnp.concatenate([halo[r, f, 2 * k], halo[r, f, 2 * k + 1]], axis=1)
+            v = dot(table, jnp.concatenate([own, got], axis=0)).astype(BF)
+            out[2 * k * slots : (2 * k + 1) * slots, :] = v[:, :side]
+            out[(2 * k + 1) * slots : (2 * k + 2) * slots, :] = v[:, side:]
+        y = HALF - 1 if f == 0 else 0
+        for zs in (range(HALF // 2), range(HALF // 2, HALF)):
+            runs = [(z, y) for z in zs]
+            for span, v in add_to(acc, runs, passes(r, src, runs, (2,))):
+                finish(span, v)
 
     lane_block = lax.broadcasted_iota(I32, (slots, width), 1) // chans
     block_f = lane_block.astype(F32).astype(BF)
@@ -346,17 +462,24 @@
             wts[r, 2, span, :] = jnp.where(is_block[w ^ 4], t[4] if vy else t[3], none)
             wts[r, 3, span, :] = jnp.where(is_block[w ^ 2], t[6] if vz else t[5], none)
 
-    pl.semaphore_wait(barrier, n - 1)
-    for f in range(4):
-        send_face(0, sig, f)
-    for r in range(3):
-        fill(r)
-    near(0, sig)
-
     def first_done(span, value):
         base[span, :] = value.astype(BF)
 
-    far(0, sig, first_done)
+    loads["fine_w"].wait()
+    fill(0)
+    near(0, sig, first_done)
+    entered()
+    for f in (0, 1, 2, 3):
+        send_face(0, sig, f)
+    for k in range(rounds):
+        if k:
+            hear(k - 1)
+        tell(k)
+        if k == 0:
+            far_z(0, sig, first_done)
+    far_y(0, sig, first_done, 1)
+    far_y(0, sig, first_done, 0)
+    hear(rounds - 1) if rounds else None
 
     sums = []
     for o in range(8):
@@ -367,6 +490,7 @@
             total = v if i == 0 else total + v
         hi = total.astype(BF)
         sums += [hi, (total - hi.astype(F32)).astype(BF)]
+    loads["same"].wait()
     sums = dot(jnp.concatenate(sums, axis=0), same[...])
     pooled = jnp.zeros((slots, width), F32)
     for o in range(8):
@@ -374,7 +498,7 @@
         pooled = jnp.where(lane_block == o, v, pooled)
     pooled = (pooled * (1.0 / HALF**3)).astype(BF)
     flat = dot(g_cell, pooled).astype(BF)
-    loads[0].wait()
+    loads["down"].wait()
     ci = jnp.zeros((cells, wide_c), F32)
     for p in range(8):
         ci = ci + jnp.dot(
@@ -385,8 +509,29 @@
     layer = cells // 2
     coarse[0] = ci[:layer]
     coarse[1] = ci[layer:]
-    stats[0:1, :] = jnp.sum(ci, axis=0, keepdims=True)
-    stats[1:2, :] = jnp.sum(ci * ci, axis=0, keepdims=True)
+    group = wide_c // GROUPS
+    lanes = stats.shape[1]
+
+    def split(v):
+        a = v.astype(BF)
+        rest = v - a.astype(F32)
+        b = rest.astype(BF)
+        return [a, b, (rest - b.astype(F32)).astype(BF)]
+
+    def in_three(v, table, dims):
+        parts = dot(jnp.concatenate([p.astype(F32) for p in split(v)], axis=0).astype(BF), table, dims)
+        tall = v.shape[0]
+        return parts[:tall] + (parts[tall : 2 * tall] + parts[2 * tall :])
+
+    grouped = (
+        lax.broadcasted_iota(I32, (wide_c, lanes), 0) // group
+        == lax.broadcasted_iota(I32, (wide_c, lanes), 1)
+    ).astype(F32).astype(BF)
+    rest = jnp.zeros((6, wide_c), F32)
+    local = jnp.concatenate(
+        [jnp.sum(ci, axis=0, keepdims=True), jnp.sum(ci * ci, axis=0, keepdims=True), rest], axis=0
+    )
+    stats[...] = in_three(local, grouped, NN)[0:2]
 
     def stat_copy(d):
         return pltpu.make_async_remote_copy(
@@ -416,7 +561,6 @@
         )
 
     lax.fori_loop(1, n, stat_go, 0)
-    low, high = mx > 0, mx < n_mx - 1
     for d in range(n_my):
         if d:
             win_copy(0, d).start()
@@ -442,13 +586,11 @@
             window[j, 3] = jnp.zeros_like(window[j, 3])
 
     pad[...] = jnp.zeros_like(pad)
-    group = wide_c // GROUPS
-    pooling = (
-        lax.broadcasted_iota(jnp.int32, (wide_c, wide_c), 0) // group
-        == lax.broadcasted_iota(jnp.int32, (wide_c, wide_c), 1) // group
-    ).astype(F32)
-    for c in loads[1:]:
-        c.wait()
+    sent_faces(0)
+    for r in (1, 2):
+        fill(r)
+    for name in ("gain", "bias", "weight", "up"):
+        loads[name].wait()
     for d in range(n_my):
         if d:
             win_copy(0, d).wait()
@@ -465,11 +607,12 @@
     lax.fori_loop(1, n, stat_wait, 0)
 
     total = float(cells * group) * n
-    sums = jnp.sum(everyone[...], axis=0)
-    sums = jnp.concatenate([sums, jnp.zeros((6, wide_c), F32)], axis=0)
-    sums = jnp.dot(sums, pooling, precision=lax.Precision.HIGHEST, preferred_element_type=F32) / total
+    sums = jnp.sum(everyone[...], axis=0) / total
     mean = sums[0:1]
     std = jnp.sqrt(sums[1:2] - mean * mean + norm_eps)
+    both_rows = jnp.concatenate([mean, std, jnp.zeros((6, lanes), F32)], axis=0)
+    both_rows = in_three(both_rows, grouped, NT)
+    mean, std = both_rows[0:1], both_rows[1:2]
     g = gain[...]
     b = bias[...]
     for zw in range(4):
@@ -533,60 +676,81 @@
         v = sums[2 * o * slots : (2 * o + 1) * slots] + sums[(2 * o + 1) * slots : (2 * o + 2) * slots]
         term[o * slots : (o + 1) * slots, :] = v
 
-    for q in range(CUBES):
-        z, y, x = q // PLANE, q // HALF % HALF, q % HALF
-        o = z // 2 * 4 + y // 2 * 2 + x // 2
-        span = slice(q * slots, (q + 1) * slots)
-        f = (base[span, :].astype(F32) + term[o * slots : (o + 1) * slots, :]).astype(BF)
-        base[span, :] = f
-        sig[span, :] = silu(f.astype(F32)).astype(BF)
-    for f in range(4):
+    def join(z, y):
+        for x in range(HALF):
+            q = (z * HALF + y) * HALF + x
+            o = z // 2 * 4 + y // 2 * 2 + x // 2
+            span = slice(q * slots, (q + 1) * slots)
+            f = (base[span, :].astype(F32) + term[o * slots : (o + 1) * slots, :]).astype(BF)
+            base[span, :] = f
+            sig[span, :] = silu(f.astype(F32)).astype(BF)
+
+    for f, y in ((0, 0), (1, HALF - 1)):
+        for z in range(HALF):
+            join(z, y)
         send_face(1, sig, f)
+    for f, z in ((2, 0), (3, HALF - 1)):
+        for y in inner:
+            join(z, y)
+        send_face(1, sig, f)
+    for z in inner:
+        for y in inner:
+            join(z, y)
 
     def second_done(span, value):
         f = value.astype(BF)
         base[span, :] = f
         sig2[span, :] = silu(f.astype(F32)).astype(BF)
 
-    near(1, sig)
-    far(1, sig, second_done)
-    for f in range(4):
+    near(1, sig, second_done)
+    far_z(1, sig, second_done)
+    for f in (1, 0):
+        far_y(1, sig, second_done, f)
+        send_face(2, sig2, f ^ 1)
+    for f in (2, 3):
         send_face(2, sig2, f)
 
     def last_done(span, value):
-        for i in range(block):
-            at = slice(i * slots, (i + 1) * slots)
-            fine[span.start + at.start : span.start + at.stop, :] = jnp.where(
-                alive, value[at], 0.0
-            ).astype(BF)
-
-    near(2, sig2)
-    far(2, sig2, last_done)
-
-
-def unfold_kernel(slots, chans, rows, coarse, sel, swap, masks, fine, coarse_out, blocks):
-    width = 8 * chans
-    side = width // 2
-    low64, low32 = masks[0] > 0.5, masks[1] > 0.5
-    for z in range(HALF):
-        for g in range(slots // 16):
+        for i in range(HALF):
+            at = slice(span.start + i * slots, span.start + (i + 1) * slots)
+            base[at, :] = jnp.where(alive, value[i * slots : (i + 1) * slots], 0.0).astype(BF)
+
+    near(2, sig2, last_done)
+    far_z(2, sig2, last_done)
+    sent_faces(1)
+    for f in (1, 0):
+        far_y(2, sig2, last_done, f)
+
+    stores = []
+    for g in range(slots // 16):
+        for z in range(HALF):
             x = jnp.concatenate(
-                [rows[(16 * z + i) * slots + 16 * g : (16 * z + i) * slots + 16 * g + 16, :]
+                [base[(16 * z + i) * slots + 16 * g : (16 * z + i) * slots + 16 * g + 16, :]
                  for i in range(16)], axis=0)
             r = dot(swap[...], x).astype(BF)
             for s in range(16):
                 at = (16 * g + s) * CUBES + 16 * z
                 blocks[at : at + 16, :] = r[16 * s : 16 * s + 16]
-    for g in range(slots // 8):
-        for h in range(2):
-            m = []
-            for s in range(8):
-                at = (8 * g + s) * CUBES + 32 * h
-                m.append((blocks[at : at + 32, :side], blocks[at : at + 32, side:]))
-            m = swap_blocks(m, low64, low32)
-            x = jnp.concatenate([jnp.concatenate(p, axis=1) for p in m], axis=0)
-            r = dot(x.T, sel[...]).astype(BF)
-            fine[8 * g : 8 * g + 8, :, 256 * h : 256 * h + 256] = r.reshape(8, chans, 256)
+        piece = pl.ds(16 * g * CUBES, 16 * CUBES)
+        stores.append(pltpu.make_async_copy(blocks.at[piece], fine.at[piece], store.at[g]))
+        stores[-1].start()
+    sent_faces(2)
+    for c in stores:
+        c.wait()
+
+
+def unfold_kernel(chans, rows, coarse, sel, masks, fine, coarse_out):
+    side = 4 * chans
+    low64, low32 = masks[0] > 0.5, masks[1] > 0.5
+    for h in range(2):
+        m = []
+        for s in range(8):
+            at = s * CUBES + 32 * h
+            m.append((rows[at : at + 32, :side], rows[at : at + 32, side:]))
+        m = swap_blocks(m, low64, low32)
+        x = jnp.concatenate([jnp.concatenate(p, axis=1) for p in m], axis=0)
+        r = dot(x.T, sel[...]).astype(BF)
+        fine[:, :, 256 * h : 256 * h + 256] = r.reshape(8, chans, 256)
     coarse_out[...] = coarse[...]
 
 
@@ -603,7 +767,11 @@
     n = n_mx * n_my
     sds = jax.ShapeDtypeStruct
     weight_t = coarse_weight.T
-    held = [pltpu.VMEM(a.shape, a.dtype) for a in (down_weight, up_weight, weight_t)]
+    ins = (
+        counts[None, :], coords, neighbours, features, fine_weights, norm_gain[None, :],
+        norm_bias[None, :], sel, swap, same, masks, down_weight, up_weight, weight_t,
+    )
+    held = [pltpu.VMEM(a.shape, a.dtype) for a in ins]
     dma = pltpu.SemaphoreType.DMA
     total = slots * CUBES
     plane = slots * PLANE
@@ -622,34 +790,36 @@
         pltpu.VMEM((3, 4, PLANE, FACE, lanes // 2), BF),
         pltpu.VMEM((8 * slots, lanes), F32),
         pltpu.VMEM((2, cells // 2, width), F32),
-        pltpu.VMEM((2, width), F32),
+        pltpu.VMEM((2, 128), F32),
         pltpu.VMEM((n_my, 4, cells // 2, width), F32),
-        pltpu.VMEM((n, 2, width), F32),
+        pltpu.VMEM((n, 2, 128), F32),
         pltpu.VMEM((4, 4, -(-(2 * n_my + 2) // 8) * 8, width), F32),
         pltpu.VMEM((n_my, cells, coarse_weight.shape[1]), F32),
         pltpu.VMEM((n_my, cells, coarse_weight.shape[1]), F32),
-        dma((3,)), dma((3, 4)), dma((3, 4)), dma((n,)), dma((n,)),
+        dma((len(ins),)), dma((3, 4)), dma((3, 4)), dma((n,)), dma((n,)),
         dma((3, n_my)), dma((3, n_my)), dma((n_my,)), dma((n_my,)),
+        pltpu.SemaphoreType.REGULAR((max(1, (n_mx - 1).bit_length()), 2)), dma((slots // 16,)),
     ]
     small = (RZ // 2, RY // 2, RX // 2, width)
     rows, coarse = pl.pallas_call(
         functools.partial(level_kernel, slots, chans, cells),
         out_shape=(sds((total, lanes), BF), sds(small, BF)),
-        in_specs=[SM] + [VM] * 10 + [pl.BlockSpec(memory_space=pl.ANY)] * 3,
-        out_specs=(VM, VM),
+        in_specs=[HBM] * len(ins),
+        out_specs=(HBM, VM),
         scratch_shapes=scratch,
         compiler_params=pltpu.CompilerParams(collective_id=0, has_side_effects=True),
-    )(
-        counts, coords, neighbours, features, fine_weights, norm_gain[None, :],
-        norm_bias[None, :], sel, swap, same, masks, down_weight, up_weight, weight_t,
-    )
+    )(*ins)
+    whole = lambda a: pl.BlockSpec(a.shape, lambda i: (0,) * a.ndim)
     return pl.pallas_call(
-        functools.partial(unfold_kernel, slots, chans),
+        functools.partial(unfold_kernel, chans),
+        grid=(slots // 8,),
         out_shape=(sds(features.shape, BF), sds(small, BF)),
-        in_specs=[VM] * 5,
-        out_specs=(VM, VM),
-        scratch_shapes=[pltpu.VMEM((total, lanes), BF)],
-    )(rows, coarse, sel, swap, masks)
+        in_specs=[pl.BlockSpec((8 * CUBES, lanes), lambda i: (i, 0))]
+        + [whole(a) for a in (coarse, sel, masks)],
+        out_specs=(
+            pl.BlockSpec((8, chans, SIDE**3), lambda i: (i, 0, 0)), whole(coarse),
+        ),
+    )(rows, coarse, sel, masks)
 
 
 def solution(mesh):

time: 41.2 us -> 41.2 us (level); the launches traced: 41 us -> 40.5 us
  Pallas kernels: 39.7 us -> 39.2 us
    pallas_call x1, Pallas kernels: 35.9 us -> 34.9 us  [local(): pl.pallas_call(functools.partial(level_kernel, slots, chans, cells), out_...]
    pallas_call x1, Pallas kernels: 3.85 us -> 4.28 us  [local(): pl.pallas_call(functools.partial(unfold_kernel, chans), grid=(slots // 8,...]
where the time goes in v2:
time: 41.2 us; the launch traced here: 40.5 us
  Pallas kernels  39.2 us (95%)
  between operations  1.29 us (3%)
    pallas_call x1, Pallas kernels, local(): pl.pallas_call(functools.partial(level_kernel, slots, chans, cells), out_...  34.9 us
    pallas_call x1, Pallas kernels, local(): pl.pallas_call(functools.partial(unfold_kernel, chans), grid=(slots // 8,...  4.28 us

profile of v2, /device:TPU:0, one launch (start us, length us, event | category | flops | bytes accessed | tf_op | source)
XLA Modules:
  0.0 40.5 jit_solution(13724904921406921406)
XLA Ops:
  1.3 34.9 %shard_map.149 = (bf16[2048,256]{1,0:T(8,128)(2,1)}, bf16[2,2,2,256]{3,2,1,0:T(2,128)(2,1)}) custom-call(s32[1,1]{1,0:T(1,128)} %bitcast.4.counts_h, s32[3,32]{1,0:T(4,128)} %coords_h.1, s32[6,32]{1,0:T(8,128)} %neighbours_h.1, bf16[32,32,512]{2,1,0:T(8,128)(2,1)} %feat_h.1, bf16[3,32,224]{2,1,0:T(8,128)(2,1)} %fine_w_h.1, f32[1,256]{1,0:T(1,128)} %bitcast.6, ...), custom_call_target="tpu_custom_call" | custom-call | tf_op jit(solution)/shard_map/pallas_call | solution.py:804
  36.2 4.3 %shard_map.150 = (bf16[32,32,512]{2,1,0:T(8,128)(2,1)}, bf16[2,2,2,256]{3,2,1,0:T(2,128)(2,1)}) custom-call(bf16[2048,256]{1,0:T(8,128)(2,1)} %get-tuple-element.4.rows, bf16[2,2,2,256]{3,2,1,0:T(2,128)(2,1)} %get-tuple-element.5.coarse, bf16[256,256]{1,0:T(8,128)(2,1)} %constant.9.clone.sel_h.sel, bf16[2,32,128]{2,1,0:T(8,128)(2,1)} %constant.8.clone.masks_h.masks), custom_call_target="tpu_custom_call" | custom-call | tf_op jit(solution)/shard_map/pallas_call | solution.py:813

commit v3 on v2

--- a/solution.py
+++ b/solution.py
@@ -46,11 +46,21 @@
     wide = np.arange(8 * chans)
     same = wide[:, None] % chans == wide[None, :] % chans
     as_bf = lambda a: jnp.asarray(np.asarray(a, np.float32), BF)
-    return as_bf(masks), as_bf(sel), as_bf(swap), as_bf(same)
+    halved = lambda a: as_bf(np.stack([a[:, :128], a[:, 128:]]))
+    return as_bf(masks), halved(sel), halved(swap), halved(same)
 
 
 def dot(a, b, dims=NN):
     return lax.dot_general(a, b, dims, preferred_element_type=F32)
+
+
+def wide_of(ref, *at):
+    return jnp.concatenate([ref[at[:-1] + (t,) + at[-1:]] for t in range(2)], axis=1)
+
+
+def keep(ref, span, value):
+    for t in range(2):
+        ref[t, span, :] = value[:, 128 * t : 128 * t + 128]
 
 
 def silu(x):
@@ -91,18 +101,30 @@
     side = width // 2
     wide_c = gain.shape[1]
 
-    order = (
-        ("feat", feat_h, feat), ("sel", sel_h, sel), ("masks", masks_h, masks),
-        ("swap", swap_h, swap), ("fine_w", fine_w_h, fine_w), ("counts", counts_h, counts),
+    chunks = feat.shape[0]
+    order = [
+        ("feat", feat_h.at[:, :, pl.ds(128 * k, 128)], feat.at[k]) for k in range(chunks)
+    ]
+    order += [
+        ("sel", sel_h, sel), ("masks", masks_h, masks), ("swap", swap_h, swap),
+        ("fine_w", fine_w_h, fine_w), ("counts", counts_h, counts),
         ("coords", coords_h, coords), ("neighbours", neighbours_h, neighbours),
-        ("same", same_h, same), ("down", down_h, down), ("gain", gain_h, gain),
-        ("bias", bias_h, bias), ("weight", weight_h, weight), ("up", up_h, up),
-    )
-    loads = {
-        name: pltpu.make_async_copy(a, b, load.at[i]) for i, (name, a, b) in enumerate(order)
-    }
-    for name, _, _ in order:
-        loads[name].start()
+    ]
+    late = [("same", same_h, same), ("gain", gain_h, gain), ("bias", bias_h, bias)]
+    late += [("down", down_h.at[:, pl.ds(128 * k, 128)], down.at[k]) for k in range(down.shape[0])]
+    late += [("weight", weight_h, weight)]
+    late += [("up", up_h.at[:, pl.ds(128 * k, 128)], up.at[k]) for k in range(up.shape[0])]
+    copies = [
+        (name, pltpu.make_async_copy(a, b, load.at[i]))
+        for i, (name, a, b) in enumerate(order + late)
+    ]
+    for _, c in copies[: len(order)]:
+        c.start()
+
+    def loaded(*names):
+        for name, c in copies:
+            if name in names:
+                c.wait()
 
     barrier = pltpu.get_barrier_semaphore()
     low, high = mx > 0, mx < n_mx - 1
@@ -148,51 +170,54 @@
         def _():
             pl.semaphore_wait(ready.at[k, 1], 1)
 
-    def where_is(d):
-        t = lax.rem(me + d, n)
-        return (t // n_my, lax.rem(t, n_my))
-
-    for name in ("feat", "sel", "masks"):
-        loads[name].wait()
+    loaded("feat", "sel", "masks")
+    for _, c in copies[len(order) :]:
+        c.start()
+
+    def at_cube(q):
+        return slice(q * slots, (q + 1) * slots)
 
     def rows(ref, q):
-        return ref[q * slots : (q + 1) * slots, :]
+        return wide_of(ref, at_cube(q))
 
     def left(ref, q):
-        return ref[q * slots : (q + 1) * slots, :side]
+        return ref[0, at_cube(q), :]
 
     def right(ref, q):
-        return ref[q * slots : (q + 1) * slots, side:]
+        return ref[1, at_cube(q), :]
+
+    def pair_of(ref):
+        return jnp.concatenate([ref[0], ref[1]], axis=1)
 
     low64, low32 = masks[0] > 0.5, masks[1] > 0.5
     zero = jnp.zeros((slots, side), BF)
 
     for g in range(slots // 8):
         for h in range(2):
-            x = feat[8 * g : 8 * g + 8, :, 256 * h : 256 * h + 256].reshape(8 * chans, 256)
-            r = dot(sel[...], x, NT).astype(BF)
+            x = jnp.concatenate(
+                [feat[2 * h + t, 8 * g : 8 * g + 8].reshape(8 * chans, 128) for t in range(2)], axis=1
+            )
+            r = dot(pair_of(sel), x, NT).astype(BF)
             m = [(r[32 * w : 32 * w + 32, :side], r[32 * w : 32 * w + 32, side:]) for w in range(8)]
             m = swap_blocks(m, low64, low32)
             for s in range(8):
                 at = (8 * g + s) * CUBES + 32 * h
-                blocks[at : at + 32, :side] = m[s][0]
-                blocks[at : at + 32, side:] = m[s][1]
-    loads["swap"].wait()
+                blocks[0, at : at + 32, :] = m[s][0]
+                blocks[1, at : at + 32, :] = m[s][1]
+    loaded("swap")
     for z in range(HALF):
         for g in range(slots // 16):
             x = jnp.concatenate(
-                [blocks[(16 * g + s) * CUBES + 16 * z : (16 * g + s) * CUBES + 16 * z + 16, :]
-                 for s in range(16)], axis=0)
-            r = dot(swap[...], x)
+                [wide_of(blocks, pl.ds((16 * g + s) * CUBES + 16 * z, 16)) for s in range(16)], axis=0)
+            r = dot(pair_of(swap), x)
             rb = r.astype(BF)
             rs = silu(r).astype(BF)
             for i in range(16):
                 at = (16 * z + i) * slots + 16 * g
-                base[at : at + 16, :] = rb[16 * i : 16 * i + 16]
-                sig[at : at + 16, :] = rs[16 * i : 16 * i + 16]
-
-    for name in ("counts", "coords", "neighbours"):
-        loads[name].wait()
+                keep(base, slice(at, at + 16), rb[16 * i : 16 * i + 16])
+                keep(sig, slice(at, at + 16), rs[16 * i : 16 * i + 16])
+
+    loaded("counts", "coords", "neighbours")
     def one_hot(row, count):
         return (lax.broadcasted_iota(I32, (count, slots), 0) == row).astype(F32).astype(BF)
 
@@ -312,7 +337,7 @@
 
     def run(ref, z, y):
         at = (z * HALF + y) * HALF * slots
-        return ref[at : at + HALF * slots, :]
+        return wide_of(ref, slice(at, at + HALF * slots))
 
     def spans(runs):
         return [
@@ -366,39 +391,41 @@
         }
         total = None
         for k in kinds:
-            v = dot(taps[k](), wts[r, k])
+            v = dot(taps[k](), jnp.concatenate([wts[r, k, 0], wts[r, k, 1]], axis=1))
             total = v if total is None else total + v
         return total
 
     def add_to(ref, runs, value):
         tall = HALF * slots
         return [
-            (span, ref[span, :].astype(F32) + value[i * tall : (i + 1) * tall])
+            (span, wide_of(ref, span).astype(F32) + value[i * tall : (i + 1) * tall])
             for i, span in enumerate(spans(runs))
         ]
 
     inner, outer = range(1, HALF - 1), (0, HALF - 1)
 
-    def near(r, src, finish):
+    def near_inner(r, src, finish):
         for zy in range(PLANE):
             first, last = halves(src, zy * HALF), halves(src, zy * HALF + HALF - 1)
             pair = jnp.concatenate(
                 [both(low32, first, (zero, zero)), both(low32, (zero, zero), last)], axis=0
             )
-            gx[zy * slots : (zy + 1) * slots, :] = dot(g_x, pair).astype(BF)
+            keep(gx, at_cube(zy), dot(g_x, pair).astype(BF))
+        for z in outer:
+            runs = [(z, y) for y in inner]
+            for span, v in add_to(base, runs, passes(r, src, runs, (0, 1, 2))):
+                keep(acc, span, v)
+        for z in inner:
+            runs = [(z, y) for y in inner]
+            for span, v in add_to(base, runs, passes(r, src, runs, (0, 1, 2, 3))):
+                finish(span, v)
+
+    def near_outer(r, src):
         for y in outer:
             for zs, kinds in ((inner, (0, 1, 3)), (outer, (0, 1))):
                 runs = [(z, y) for z in zs]
                 for span, v in add_to(base, runs, passes(r, src, runs, kinds)):
-                    acc[span, :] = v
-        for z in outer:
-            runs = [(z, y) for y in inner]
-            for span, v in add_to(base, runs, passes(r, src, runs, (0, 1, 2))):
-                acc[span, :] = v
-        for z in inner:
-            runs = [(z, y) for y in inner]
-            for span, v in add_to(base, runs, passes(r, src, runs, (0, 1, 2, 3))):
-                finish(span, v)
+                    keep(acc, span, v)
 
     def far_z(r, src, finish):
         for f in (2, 3):
@@ -411,7 +438,7 @@
                     [both(low64, first, (zero, zero)), z_halo(r, 2, y, x),
                      both(low64, (zero, zero), last), z_halo(r, 3, y, x)], axis=0,
                 )
-                gz[i * slots : (i + 1) * slots, :] = dot(g_z, both_z).astype(BF)
+                keep(gz, at_cube(i), dot(g_z, both_z).astype(BF))
         for z in outer:
             runs = [(z, y) for y in inner]
             for span, v in add_to(acc, runs, passes(r, src, runs, (3,))):
@@ -419,7 +446,7 @@
         for y in outer:
             runs = [(z, y) for z in outer]
             for span, v in add_to(acc, runs, passes(r, src, runs, (3,))):
-                acc[span, :] = v
+                keep(acc, span, v)
 
     def far_y(r, src, finish, f):
         take_face(r, f)
@@ -447,6 +474,10 @@
     none = jnp.zeros((chans, width), BF)
     is_block = [block_f == float(w) for w in range(8)]
 
+    def fit(r, k, span, v):
+        for t in range(2):
+            wts[r, k, t, span, :] = v[:, side * t : side * t + side]
+
     def fill(r):
         t = dot(fine_w[r], spread, TN).astype(BF)
         t = [t[i * chans : (i + 1) * chans] for i in range(7)]
@@ -457,29 +488,32 @@
             v = jnp.where(is_block[w ^ 1], t[1] if vx else t[2], v)
             v = jnp.where(is_block[w ^ 4], t[3] if vy else t[4], v)
             v = jnp.where(is_block[w ^ 2], t[5] if vz else t[6], v)
-            wts[r, 0, span, :] = v
-            wts[r, 1, span, :] = jnp.where(is_block[w ^ 1], t[2] if vx else t[1], none)
-            wts[r, 2, span, :] = jnp.where(is_block[w ^ 4], t[4] if vy else t[3], none)
-            wts[r, 3, span, :] = jnp.where(is_block[w ^ 2], t[6] if vz else t[5], none)
+            fit(r, 0, span, v)
+            fit(r, 1, span, jnp.where(is_block[w ^ 1], t[2] if vx else t[1], none))
+            fit(r, 2, span, jnp.where(is_block[w ^ 4], t[4] if vy else t[3], none))
+            fit(r, 3, span, jnp.where(is_block[w ^ 2], t[6] if vz else t[5], none))
 
     def first_done(span, value):
-        base[span, :] = value.astype(BF)
-
-    loads["fine_w"].wait()
+        keep(base, span, value.astype(BF))
+
+    loaded("fine_w")
     fill(0)
-    near(0, sig, first_done)
+    near_inner(0, sig, first_done)
     entered()
     for f in (0, 1, 2, 3):
         send_face(0, sig, f)
-    for k in range(rounds):
-        if k:
-            hear(k - 1)
+    if rounds:
+        tell(0)
+    near_outer(0, sig)
+    for k in range(1, rounds):
+        hear(k - 1)
         tell(k)
-        if k == 0:
+        if k == 1:
             far_z(0, sig, first_done)
+    if rounds < 2:
+        far_z(0, sig, first_done)
     far_y(0, sig, first_done, 1)
     far_y(0, sig, first_done, 0)
-    hear(rounds - 1) if rounds else None
 
     sums = []
     for o in range(8):
@@ -490,20 +524,20 @@
             total = v if i == 0 else total + v
         hi = total.astype(BF)
         sums += [hi, (total - hi.astype(F32)).astype(BF)]
-    loads["same"].wait()
-    sums = dot(jnp.concatenate(sums, axis=0), same[...])
+    loaded("same")
+    sums = dot(jnp.concatenate(sums, axis=0), pair_of(same))
     pooled = jnp.zeros((slots, width), F32)
     for o in range(8):
         v = sums[2 * o * slots : (2 * o + 1) * slots] + sums[(2 * o + 1) * slots : (2 * o + 2) * slots]
         pooled = jnp.where(lane_block == o, v, pooled)
     pooled = (pooled * (1.0 / HALF**3)).astype(BF)
     flat = dot(g_cell, pooled).astype(BF)
-    loads["down"].wait()
+    loaded("down")
     ci = jnp.zeros((cells, wide_c), F32)
     for p in range(8):
         ci = ci + jnp.dot(
             flat[p * cells : (p + 1) * cells],
-            down[p * width : (p + 1) * width, :],
+            jnp.concatenate([down[t, p * width : (p + 1) * width, :] for t in range(down.shape[0])], axis=1),
             preferred_element_type=F32,
         )
     layer = cells // 2
@@ -533,19 +567,15 @@
     )
     stats[...] = in_three(local, grouped, NN)[0:2]
 
-    def stat_copy(d):
+    offsets = sorted(range(n_mx), key=lambda i: -min(i, n_mx - i))
+    others = [(i, j) for i in offsets for j in range(n_my) if i or j]
+
+    def stat_copy(i, j):
+        d = i * n_my + j
         return pltpu.make_async_remote_copy(
             src_ref=stats, dst_ref=everyone.at[me], send_sem=ssend.at[d], recv_sem=srecv.at[d],
-            device_id=where_is(d), device_id_type=MESH,
+            device_id=(lax.rem(mx + i, n_mx), lax.rem(my + j, n_my)), device_id_type=MESH,
         )
-
-    def stat_go(d, c):
-        stat_copy(d).start()
-        return c
-
-    def stat_wait(d, c):
-        stat_copy(d).wait()
-        return c
 
     def win_copy(kind, d):
         t = lax.rem(my + d, n_my)
@@ -560,7 +590,10 @@
             device_id=(a, t), device_id_type=MESH,
         )
 
-    lax.fori_loop(1, n, stat_go, 0)
+    if rounds:
+        hear(rounds - 1)
+    for i, j in others:
+        stat_copy(i, j).start()
     for d in range(n_my):
         if d:
             win_copy(0, d).start()
@@ -589,8 +622,7 @@
     sent_faces(0)
     for r in (1, 2):
         fill(r)
-    for name in ("gain", "bias", "weight", "up"):
-        loads[name].wait()
+    loaded("gain", "bias", "weight", "up")
     for d in range(n_my):
         if d:
             win_copy(0, d).wait()
@@ -604,7 +636,8 @@
         def _():
             win_copy(2, d).wait_send()
             win_copy(1, d).wait_recv()
-    lax.fori_loop(1, n, stat_wait, 0)
+    for i, j in others:
+        stat_copy(i, j).wait()
 
     total = float(cells * group) * n
     sums = jnp.sum(everyone[...], axis=0) / total
@@ -665,13 +698,13 @@
             q = z * 4 + y
             pair = jnp.concatenate([cof[q : q + 1], cof[q + 2 : q + 3]], axis=0)
             coarse_out[z, y] = pair.astype(BF)
-    wide = jnp.dot(co, up[...], preferred_element_type=F32)
+    wide = dot(co, jnp.concatenate([up[k] for k in range(up.shape[0])], axis=1))
     lifted = jnp.concatenate([wide[:, p * width : (p + 1) * width] for p in range(8)], axis=0)
     hi = lifted.astype(BF)
     lo = (lifted - hi.astype(F32)).astype(BF)
     picked = [dot(g_lift, v).astype(BF) for v in (hi, lo)]
     spots = [jnp.where(is_block[o], v, jnp.zeros_like(v)) for o in range(8) for v in picked]
-    sums = dot(jnp.concatenate(spots, axis=0), same[...])
+    sums = dot(jnp.concatenate(spots, axis=0), pair_of(same))
     for o in range(8):
         v = sums[2 * o * slots : (2 * o + 1) * slots] + sums[(2 * o + 1) * slots : (2 * o + 2) * slots]
         term[o * slots : (o + 1) * slots, :] = v
@@ -681,9 +714,9 @@
             q = (z * HALF + y) * HALF + x
             o = z // 2 * 4 + y // 2 * 2 + x // 2
             span = slice(q * slots, (q + 1) * slots)
-            f = (base[span, :].astype(F32) + term[o * slots : (o + 1) * slots, :]).astype(BF)
-            base[span, :] = f
-            sig[span, :] = silu(f.astype(F32)).astype(BF)
+            f = (wide_of(base, span).astype(F32) + term[o * slots : (o + 1) * slots, :]).astype(BF)
+            keep(base, span, f)
+            keep(sig, span, silu(f.astype(F32)).astype(BF))
 
     for f, y in ((0, 0), (1, HALF - 1)):
         for z in range(HALF):
@@ -699,10 +732,11 @@
 
     def second_done(span, value):
         f = value.astype(BF)
-        base[span, :] = f
-        sig2[span, :] = silu(f.astype(F32)).astype(BF)
-
-    near(1, sig, second_done)
+        keep(base, span, f)
+        keep(sig2, span, silu(f.astype(F32)).astype(BF))
+
+    near_inner(1, sig, second_done)
+    near_outer(1, sig)
     far_z(1, sig, second_done)
     for f in (1, 0):
         far_y(1, sig, second_done, f)
@@ -713,9 +747,10 @@
     def last_done(span, value):
         for i in range(HALF):
             at = slice(span.start + i * slots, span.start + (i + 1) * slots)
-            base[at, :] = jnp.where(alive, value[i * slots : (i + 1) * slots], 0.0).astype(BF)
-
-    near(2, sig2, last_done)
+            keep(base, at, jnp.where(alive, value[i * slots : (i + 1) * slots], 0.0).astype(BF))
+
+    near_inner(2, sig2, last_done)
+    near_outer(2, sig2)
     far_z(2, sig2, last_done)
     sent_faces(1)
     for f in (1, 0):
@@ -725,13 +760,12 @@
     for g in range(slots // 16):
         for z in range(HALF):
             x = jnp.concatenate(
-                [base[(16 * z + i) * slots + 16 * g : (16 * z + i) * slots + 16 * g + 16, :]
-                 for i in range(16)], axis=0)
-            r = dot(swap[...], x).astype(BF)
+                [wide_of(base, pl.ds((16 * z + i) * slots + 16 * g, 16)) for i in range(16)], axis=0)
+            r = dot(pair_of(swap), x).astype(BF)
             for s in range(16):
                 at = (16 * g + s) * CUBES + 16 * z
-                blocks[at : at + 16, :] = r[16 * s : 16 * s + 16]
-        piece = pl.ds(16 * g * CUBES, 16 * CUBES)
+                keep(blocks, slice(at, at + 16), r[16 * s : 16 * s + 16])
+        piece = (slice(None), pl.ds(16 * g * CUBES, 16 * CUBES))
         stores.append(pltpu.make_async_copy(blocks.at[piece], fine.at[piece], store.at[g]))
         stores[-1].start()
     sent_faces(2)
@@ -740,16 +774,15 @@
 
 
 def unfold_kernel(chans, rows, coarse, sel, masks, fine, coarse_out):
-    side = 4 * chans
     low64, low32 = masks[0] > 0.5, masks[1] > 0.5
     for h in range(2):
         m = []
         for s in range(8):
             at = s * CUBES + 32 * h
-            m.append((rows[at : at + 32, :side], rows[at : at + 32, side:]))
+            m.append((rows[0, at : at + 32, :], rows[1, at : at + 32, :]))
         m = swap_blocks(m, low64, low32)
         x = jnp.concatenate([jnp.concatenate(p, axis=1) for p in m], axis=0)
-        r = dot(x.T, sel[...]).astype(BF)
+        r = dot(x.T, jnp.concatenate([sel[0], sel[1]], axis=1)).astype(BF)
         fine[:, :, 256 * h : 256 * h + 256] = r.reshape(8, chans, 256)
     coarse_out[...] = coarse[...]
 
@@ -772,20 +805,23 @@
         norm_bias[None, :], sel, swap, same, masks, down_weight, up_weight, weight_t,
     )
     held = [pltpu.VMEM(a.shape, a.dtype) for a in ins]
+    held[3] = pltpu.VMEM((SIDE**3 // 128, slots, chans, 128), BF)
+    held[11] = pltpu.VMEM((width // 128, down_weight.shape[0], 128), BF)
+    held[12] = pltpu.VMEM((up_weight.shape[1] // 128, width, 128), BF)
     dma = pltpu.SemaphoreType.DMA
     total = slots * CUBES
     plane = slots * PLANE
     scratch = held + [
-        pltpu.VMEM((total, lanes), BF),
-        pltpu.VMEM((total, lanes), BF),
-        pltpu.VMEM((total, lanes), BF),
-        pltpu.VMEM((total, lanes), BF),
-        pltpu.VMEM((total, lanes), F32),
-        pltpu.VMEM((3, 4, lanes, lanes), BF),
-        pltpu.VMEM((plane, lanes), BF),
+        pltpu.VMEM((2, total, 128), BF),
+        pltpu.VMEM((2, total, 128), BF),
+        pltpu.VMEM((2, total, 128), BF),
+        pltpu.VMEM((2, total, 128), BF),
+        pltpu.VMEM((2, total, 128), F32),
+        pltpu.VMEM((3, 4, 2, lanes, 128), BF),
+        pltpu.VMEM((2, plane, 128), BF),
         pltpu.VMEM((plane, lanes // 2), BF),
         pltpu.VMEM((plane, lanes // 2), BF),
-        pltpu.VMEM((plane, lanes), BF),
+        pltpu.VMEM((2, plane, 128), BF),
         pltpu.VMEM((3, 4, PLANE, FACE, lanes // 2), BF),
         pltpu.VMEM((3, 4, PLANE, FACE, lanes // 2), BF),
         pltpu.VMEM((8 * slots, lanes), F32),
@@ -796,14 +832,14 @@
         pltpu.VMEM((4, 4, -(-(2 * n_my + 2) // 8) * 8, width), F32),
         pltpu.VMEM((n_my, cells, coarse_weight.shape[1]), F32),
         pltpu.VMEM((n_my, cells, coarse_weight.shape[1]), F32),
-        dma((len(ins),)), dma((3, 4)), dma((3, 4)), dma((n,)), dma((n,)),
+        dma((64,)), dma((3, 4)), dma((3, 4)), dma((n,)), dma((n,)),
         dma((3, n_my)), dma((3, n_my)), dma((n_my,)), dma((n_my,)),
         pltpu.SemaphoreType.REGULAR((max(1, (n_mx - 1).bit_length()), 2)), dma((slots // 16,)),
     ]
     small = (RZ // 2, RY // 2, RX // 2, width)
     rows, coarse = pl.pallas_call(
         functools.partial(level_kernel, slots, chans, cells),
-        out_shape=(sds((total, lanes), BF), sds(small, BF)),
+        out_shape=(sds((2, total, 128), BF), sds(small, BF)),
         in_specs=[HBM] * len(ins),
         out_specs=(HBM, VM),
         scratch_shapes=scratch,
@@ -814,7 +850,7 @@
         functools.partial(unfold_kernel, chans),
         grid=(slots // 8,),
         out_shape=(sds(features.shape, BF), sds(small, BF)),
-        in_specs=[pl.BlockSpec((8 * CUBES, lanes), lambda i: (i, 0))]
+        in_specs=[pl.BlockSpec((2, 8 * CUBES, 128), lambda i: (0, i, 0))]
         + [whole(a) for a in (coarse, sel, masks)],
         out_specs=(
             pl.BlockSpec((8, chans, SIDE**3), lambda i: (i, 0, 0)), whole(coarse),

time: 41.2 us -> 41.1 us (level)
  no operation moved by 1% of the time
where the time goes in v3:
time: 41.1 us; the launch traced here: 40.4 us
  Pallas kernels  39.1 us (95%)
  between operations  1.29 us (3%)
    pallas_call x1, Pallas kernels, local(): pl.pallas_call(functools.partial(level_kernel, slots, chans, cells), out_...  34.8 us
    pallas_call x1, Pallas kernels, local(): pl.pallas_call(functools.partial(unfold_kernel, chans), grid=(slots // 8,...  4.28 us

profile of v3, /device:TPU:0, one launch (start us, length us, event | category | flops | bytes accessed | tf_op | source)
XLA Modules:
  0.0 40.4 jit_solution(7004257549193414797)
XLA Ops:
  1.3 34.8 %shard_map.149 = (bf16[2,2048,128]{2,1,0:T(8,128)(2,1)}, bf16[2,2,2,256]{3,2,1,0:T(2,128)(2,1)}) custom-call(s32[1,1]{1,0:T(1,128)} %bitcast.4.counts_h, s32[3,32]{1,0:T(4,128)} %coords_h.1, s32[6,32]{1,0:T(8,128)} %neighbours_h.1, bf16[32,32,512]{2,1,0:T(8,128)(2,1)} %feat_h.1, bf16[3,32,224]{2,1,0:T(8,128)(2,1)} %fine_w_h.1, f32[1,256]{1,0:T(1,128)} %bitcast.6, ...), custom_call_target="tpu_custom_call" | custom-call | tf_op jit(solution)/shard_map/pallas_call | solution.py:840
  36.1 4.3 %shard_map.150 = (bf16[32,32,512]{2,1,0:T(8,128)(2,1)}, bf16[2,2,2,256]{3,2,1,0:T(2,128)(2,1)}) custom-call(bf16[2,2048,128]{2,1,0:T(8,128)(2,1)} %get-tuple-element.4.rows, bf16[2,2,2,256]{3,2,1,0:T(2,128)(2,1)} %get-tuple-element.5.coarse, bf16[2,256,128]{2,1,0:T(8,128)(2,1)} %constant.9.clone.sel_h.sel, bf16[2,32,128]{2,1,0:T(8,128)(2,1)} %constant.8.clone.masks_h.masks), custom_call_target="tpu_custom_call" | custom-call | tf_op jit(solution)/shard_map/pallas_call | solution.py:849

commit v4 on v3

--- a/solution.py
+++ b/solution.py
@@ -91,7 +91,7 @@
     counts, coords, neighbours, feat, fine_w, gain, bias, sel, swap, same, masks, down, up, weight,
     blocks, base, sig, sig2, acc, wts, gx, gyp, gym, gz, faces, halo, term,
     coarse, stats, window, everyone, pad, part, result,
-    load, fsend, frecv, ssend, srecv, wsend, wrecv, rsend, rrecv, ready, store,
+    load, fsend, frecv, ssend, srecv, wsend, wrecv, rsend, rrecv, ready,
 ):
     n_mx, n_my = lax.axis_size("mx"), lax.axis_size("my")
     mx, my = lax.axis_index("mx"), lax.axis_index("my")
@@ -496,14 +496,14 @@
     def first_done(span, value):
         keep(base, span, value.astype(BF))
 
-    loaded("fine_w")
-    fill(0)
-    near_inner(0, sig, first_done)
     entered()
     for f in (0, 1, 2, 3):
         send_face(0, sig, f)
     if rounds:
         tell(0)
+    loaded("fine_w")
+    fill(0)
+    near_inner(0, sig, first_done)
     near_outer(0, sig)
     for k in range(1, rounds):
         hear(k - 1)
@@ -756,7 +756,7 @@
     for f in (1, 0):
         far_y(2, sig2, last_done, f)
 
-    stores = []
+    sent_faces(2)
     for g in range(slots // 16):
         for z in range(HALF):
             x = jnp.concatenate(
@@ -764,27 +764,37 @@
             r = dot(pair_of(swap), x).astype(BF)
             for s in range(16):
                 at = (16 * g + s) * CUBES + 16 * z
-                keep(blocks, slice(at, at + 16), r[16 * s : 16 * s + 16])
-        piece = (slice(None), pl.ds(16 * g * CUBES, 16 * CUBES))
-        stores.append(pltpu.make_async_copy(blocks.at[piece], fine.at[piece], store.at[g]))
+                keep(fine, slice(at, at + 16), r[16 * s : 16 * s + 16])
+
+
+def unfold_kernel(chans, slots, rows, coarse, sel_h, masks_h, fine_h, coarse_h, sel, masks, fine, kept, sem):
+    loads = [
+        pltpu.make_async_copy(a, b, sem.at[i])
+        for i, (a, b) in enumerate(((sel_h, sel), (masks_h, masks)))
+    ]
+    for c in loads:
+        c.start()
+    kept[...] = coarse[...]
+    for c in loads:
+        c.wait()
+    stores = [pltpu.make_async_copy(kept, coarse_h, sem.at[2])]
+    stores[0].start()
+    low64, low32 = masks[0] > 0.5, masks[1] > 0.5
+    for g in range(slots // 8):
+        for h in range(2):
+            m = []
+            for s in range(8):
+                at = (8 * g + s) * CUBES + 32 * h
+                m.append((rows[0, at : at + 32, :], rows[1, at : at + 32, :]))
+            m = swap_blocks(m, low64, low32)
+            x = jnp.concatenate([jnp.concatenate(p, axis=1) for p in m], axis=0)
+            r = dot(x.T, jnp.concatenate([sel[0], sel[1]], axis=1)).astype(BF)
+            fine[8 * g : 8 * g + 8, :, 256 * h : 256 * h + 256] = r.reshape(8, chans, 256)
+        part = pl.ds(8 * g, 8)
+        stores.append(pltpu.make_async_copy(fine.at[part], fine_h.at[part], sem.at[3 + g]))
         stores[-1].start()
-    sent_faces(2)
     for c in stores:
         c.wait()
-
-
-def unfold_kernel(chans, rows, coarse, sel, masks, fine, coarse_out):
-    low64, low32 = masks[0] > 0.5, masks[1] > 0.5
-    for h in range(2):
-        m = []
-        for s in range(8):
-            at = s * CUBES + 32 * h
-            m.append((rows[0, at : at + 32, :], rows[1, at : at + 32, :]))
-        m = swap_blocks(m, low64, low32)
-        x = jnp.concatenate([jnp.concatenate(p, axis=1) for p in m], axis=0)
-        r = dot(x.T, jnp.concatenate([sel[0], sel[1]], axis=1)).astype(BF)
-        fine[:, :, 256 * h : 256 * h + 256] = r.reshape(8, chans, 256)
-    coarse_out[...] = coarse[...]
 
 
 def local(
@@ -834,28 +844,27 @@
         pltpu.VMEM((n_my, cells, coarse_weight.shape[1]), F32),
         dma((64,)), dma((3, 4)), dma((3, 4)), dma((n,)), dma((n,)),
         dma((3, n_my)), dma((3, n_my)), dma((n_my,)), dma((n_my,)),
-        pltpu.SemaphoreType.REGULAR((max(1, (n_mx - 1).bit_length()), 2)), dma((slots // 16,)),
+        pltpu.SemaphoreType.REGULAR((max(1, (n_mx - 1).bit_length()), 2)),
     ]
     small = (RZ // 2, RY // 2, RX // 2, width)
     rows, coarse = pl.pallas_call(
         functools.partial(level_kernel, slots, chans, cells),
-        out_shape=(sds((2, total, 128), BF), sds(small, BF)),
+        out_shape=(pltpu.VMEM((2, total, 128), BF), pltpu.VMEM(small, BF)),
         in_specs=[HBM] * len(ins),
-        out_specs=(HBM, VM),
+        out_specs=(VM, VM),
         scratch_shapes=scratch,
         compiler_params=pltpu.CompilerParams(collective_id=0, has_side_effects=True),
     )(*ins)
-    whole = lambda a: pl.BlockSpec(a.shape, lambda i: (0,) * a.ndim)
     return pl.pallas_call(
-        functools.partial(unfold_kernel, chans),
-        grid=(slots // 8,),
+        functools.partial(unfold_kernel, chans, slots),
         out_shape=(sds(features.shape, BF), sds(small, BF)),
-        in_specs=[pl.BlockSpec((2, 8 * CUBES, 128), lambda i: (0, i, 0))]
-        + [whole(a) for a in (coarse, sel, masks)],
-        out_specs=(
-            pl.BlockSpec((8, chans, SIDE**3), lambda i: (i, 0, 0)), whole(coarse),
-        ),
-    )(rows, coarse, sel, masks)
+        in_specs=[VM, VM, HBM, HBM],
+        out_specs=(HBM, HBM),
+        scratch_shapes=[
+            pltpu.VMEM(sel.shape, BF), pltpu.VMEM(masks.shape, BF), pltpu.VMEM(features.shape, BF),
+            pltpu.VMEM(small, BF), dma((3 + slots // 8,)),
+        ],
+    )(*[pltpu.with_memory_space_constraint(a, pltpu.VMEM) for a in (rows, coarse)], sel, masks)
 
 
 def solution(mesh):

time: 41.1 us -> 37.9 us (0.922)
  Pallas kernels: 39.1 us -> 35.8 us
    pallas_call x1, Pallas kernels: 34.8 us -> 32.5 us  [local(): pl.pallas_call(functools.partial(level_kernel, slots, chans, cells), out_...]
    pallas_call x1, Pallas kernels: 4.28 us -> 3.33 us  [local(): pl.pallas_call(functools.partial(unfold_kernel, chans, slots), out_shape=...]
where the time goes in v4:
time: 37.9 us; the launch traced here: 37.3 us
  Pallas kernels  35.8 us (94%)
  between operations  1.45 us (4%)
    pallas_call x1, Pallas kernels, local(): pl.pallas_call(functools.partial(level_kernel, slots, chans, cells), out_...  32.5 us
    pallas_call x1, Pallas kernels, local(): pl.pallas_call(functools.partial(unfold_kernel, chans, slots), out_shape=...  3.33 us

profile of v4, /device:TPU:0, one launch (start us, length us, event | category | flops | bytes accessed | tf_op | source)
XLA Modules:
  0.0 37.3 jit_solution(7566294046798672855)
XLA Ops:
  1.3 32.5 %shard_map.149 = (bf16[2,2048,128]{2,1,0:T(8,128)(2,1)S(1)}, bf16[2,2,2,256]{3,2,1,0:T(2,128)(2,1)S(1)}) custom-call(s32[1,1]{1,0:T(1,128)} %bitcast.4.counts_h, s32[3,32]{1,0:T(4,128)} %coords_h.1, s32[6,32]{1,0:T(8,128)} %neighbours_h.1, bf16[32,32,512]{2,1,0:T(8,128)(2,1)} %feat_h.1, bf16[3,32,224]{2,1,0:T(8,128)(2,1)} %fine_w_h.1, f32[1,256]{1,0:T(1,128)} %bitcast.6, ...), custom_call_target="tpu_custom_call" | custom-call | tf_op jit(solution)/shard_map/pallas_call | solution.py:850
  33.8 3.3 %shard_map.150 = (bf16[32,32,512]{2,1,0:T(8,128)(2,1)}, bf16[2,2,2,256]{3,2,1,0:T(2,128)(2,1)}) custom-call(bf16[2,2048,128]{2,1,0:T(8,128)(2,1)S(1)} %get-tuple-element.4.rows, bf16[2,2,2,256]{3,2,1,0:T(2,128)(2,1)S(1)} %get-tuple-element.5.coarse, bf16[2,256,128]{2,1,0:T(8,128)(2,1)} %constant.9.clone.sel_h, bf16[2,32,128]{2,1,0:T(8,128)(2,1)} %constant.8.clone.masks_h), custom_call_target="tpu_custom_call" | custom-call | tf_op jit(solution)/shard_map/pallas_call | solution.py:858

commit v5 on v4

--- a/solution.py
+++ b/solution.py
@@ -87,7 +87,7 @@
     slots, chans, cells,
     counts_h, coords_h, neighbours_h, feat_h, fine_w_h, gain_h, bias_h, sel_h, swap_h, same_h,
     masks_h, down_h, up_h, weight_h,
-    fine, coarse_out,
+    fine, coarse_out, sel_out, masks_out,
     counts, coords, neighbours, feat, fine_w, gain, bias, sel, swap, same, masks, down, up, weight,
     blocks, base, sig, sig2, acc, wts, gx, gyp, gym, gz, faces, halo, term,
     coarse, stats, window, everyone, pad, part, result,
@@ -427,7 +427,7 @@
                 for span, v in add_to(base, runs, passes(r, src, runs, kinds)):
                     keep(acc, span, v)
 
-    def far_z(r, src, finish):
+    def gather_z(r, src):
         for f in (2, 3):
             take_face(r, f)
         for y in range(HALF):
@@ -439,17 +439,8 @@
                      both(low64, (zero, zero), last), z_halo(r, 3, y, x)], axis=0,
                 )
                 keep(gz, at_cube(i), dot(g_z, both_z).astype(BF))
-        for z in outer:
-            runs = [(z, y) for y in inner]
-            for span, v in add_to(acc, runs, passes(r, src, runs, (3,))):
-                finish(span, v)
-        for y in outer:
-            runs = [(z, y) for z in outer]
-            for span, v in add_to(acc, runs, passes(r, src, runs, (3,))):
-                keep(acc, span, v)
-
-    def far_y(r, src, finish, f):
-        take_face(r, f)
+
+    def gather_y(r, src, f):
         part_of, table, out = ((left, g_yp, gyp), (right, g_ym, gym))[f]
         for k in range(PLANE // 2):
             z, x = k // 2, k % 2 * 2
@@ -459,11 +450,27 @@
             v = dot(table, jnp.concatenate([own, got], axis=0)).astype(BF)
             out[2 * k * slots : (2 * k + 1) * slots, :] = v[:, :side]
             out[(2 * k + 1) * slots : (2 * k + 2) * slots, :] = v[:, side:]
+
+    def more(r, src, runs, kind, finish=None):
+        for span, v in add_to(acc, runs, passes(r, src, runs, (kind,))):
+            if finish is None:
+                keep(acc, span, v)
+            else:
+                finish(span, v)
+
+    def far_z(r, src, finish):
+        gather_z(r, src)
+        for z in outer:
+            more(r, src, [(z, y) for y in inner], 3, finish)
+        for y in outer:
+            more(r, src, [(z, y) for z in outer], 3)
+
+    def far_y(r, src, finish, f):
+        take_face(r, f)
+        gather_y(r, src, f)
         y = HALF - 1 if f == 0 else 0
         for zs in (range(HALF // 2), range(HALF // 2, HALF)):
-            runs = [(z, y) for z in zs]
-            for span, v in add_to(acc, runs, passes(r, src, runs, (2,))):
-                finish(span, v)
+            more(r, src, [(z, y) for z in zs], 2, finish)
 
     lane_block = lax.broadcasted_iota(I32, (slots, width), 1) // chans
     block_f = lane_block.astype(F32).astype(BF)
@@ -513,7 +520,9 @@
     if rounds < 2:
         far_z(0, sig, first_done)
     far_y(0, sig, first_done, 1)
+    send_face(1, base, 0)
     far_y(0, sig, first_done, 0)
+    send_face(1, base, 1)
 
     sums = []
     for o in range(8):
@@ -619,6 +628,8 @@
             window[j, 3] = jnp.zeros_like(window[j, 3])
 
     pad[...] = jnp.zeros_like(pad)
+    sel_out[...] = sel[...]
+    masks_out[...] = masks[...]
     sent_faces(0)
     for r in (1, 2):
         fill(r)
@@ -675,6 +686,9 @@
     for j in range(n_my):
         for zx in range(4):
             part[j, 2 * zx : 2 * zx + 2, :] = sums[zx * tall + 2 * j : zx * tall + 2 * j + 2, :]
+            above, below = zx * tall + 2 * min(j + 1, n_my - 1), zx * tall + 2 * max(j - 1, 0) + 1
+            part[j, cells + zx : cells + zx + 1, :] = sums[above : above + 1, :]
+            part[j, cells + 4 + zx : cells + 5 + zx, :] = sums[below : below + 1, :]
     copies = []
     for d in range(1, n_my):
         to = lax.rem(my + d, n_my)
@@ -691,7 +705,12 @@
         c.wait()
 
     whole = jnp.concatenate([result[j] for j in range(n_my)], axis=1)
-    co = (whole + jnp.concatenate([coarse[0], coarse[1]], axis=0)).astype(BF)
+    above, below = jnp.minimum(my + 1, n_my - 1), jnp.maximum(my - 1, 0)
+    beside = [window[above, 1], window[above, 2], window[below, 1], window[below, 2]]
+    beside = [
+        v[r : r + 1] for i, v in enumerate(beside) for r in ((0, 2) if i < 2 else (1, 3))
+    ]
+    co = (whole + jnp.concatenate([coarse[0], coarse[1]] + beside, axis=0)).astype(BF)
     cof = co.astype(F32)
     for z in range(2):
         for y in range(2):
@@ -699,11 +718,30 @@
             pair = jnp.concatenate([cof[q : q + 1], cof[q + 2 : q + 3]], axis=0)
             coarse_out[z, y] = pair.astype(BF)
     wide = dot(co, jnp.concatenate([up[k] for k in range(up.shape[0])], axis=1))
-    lifted = jnp.concatenate([wide[:, p * width : (p + 1) * width] for p in range(8)], axis=0)
-    hi = lifted.astype(BF)
-    lo = (lifted - hi.astype(F32)).astype(BF)
-    picked = [dot(g_lift, v).astype(BF) for v in (hi, lo)]
+    def in_two(v):
+        hi = v.astype(BF)
+        return hi, (v - hi.astype(F32)).astype(BF)
+
+    def lifted(at):
+        return jnp.concatenate(
+            [wide[at : at + cells, p * width : (p + 1) * width] for p in range(8)], axis=0
+        )
+
+    picked = [dot(g_lift, v).astype(BF) for v in in_two(lifted(0))]
     spots = [jnp.where(is_block[o], v, jnp.zeros_like(v)) for o in range(8) for v in picked]
+
+    k = lax.broadcasted_iota(I32, (2 * FACE, 8 * cells), 0)
+    down_side = k // FACE
+    kz, kx = k % FACE // RX, k % RX
+    row = (kz % 2 * 4 + down_side * 2 + kx % 2) * cells + down_side * 4 + kz // 2 * 2 + kx // 2
+    g_halo = (lax.broadcasted_iota(I32, (2 * FACE, 8 * cells), 1) == row).astype(F32).astype(BF)
+    picked = [dot(g_halo, v).astype(BF) for v in in_two(lifted(cells))]
+    for zx in range(4):
+        for v in picked:
+            for f in range(2):
+                o = zx // 2 * 4 + f * 2 + zx % 2
+                v_f = v[f * FACE : (f + 1) * FACE]
+                spots.append(jnp.where(is_block[o][:FACE], v_f, jnp.zeros_like(v_f)))
     sums = dot(jnp.concatenate(spots, axis=0), pair_of(same))
     for o in range(8):
         v = sums[2 * o * slots : (2 * o + 1) * slots] + sums[(2 * o + 1) * slots : (2 * o + 2) * slots]
@@ -718,17 +756,20 @@
             keep(base, span, f)
             keep(sig, span, silu(f.astype(F32)).astype(BF))
 
-    for f, y in ((0, 0), (1, HALF - 1)):
-        for z in range(HALF):
-            join(z, y)
-        send_face(1, sig, f)
     for f, z in ((2, 0), (3, HALF - 1)):
-        for y in inner:
+        for y in range(HALF):
             join(z, y)
         send_face(1, sig, f)
     for z in inner:
-        for y in inner:
+        for y in range(HALF):
             join(z, y)
+    for f in range(2):
+        take_face(1, f)
+        for zx in range(PLANE):
+            at = 16 * slots + (zx // 8 * 2 + zx % 4 // 2) * 4 * FACE + f * FACE
+            lift = sums[at : at + FACE, :side] + sums[at + 2 * FACE : at + 3 * FACE, :side]
+            v = (halo[1, f, zx].astype(F32) + lift).astype(BF)
+            halo[1, f, zx] = silu(v.astype(F32)).astype(BF)
 
     def second_done(span, value):
         f = value.astype(BF)
@@ -737,11 +778,16 @@
 
     near_inner(1, sig, second_done)
     near_outer(1, sig)
-    far_z(1, sig, second_done)
-    for f in (1, 0):
-        far_y(1, sig, second_done, f)
-        send_face(2, sig2, f ^ 1)
-    for f in (2, 3):
+    for f, y in ((1, 0), (0, HALF - 1)):
+        gather_y(1, sig, f)
+        more(1, sig, [(z, y) for z in inner], 2, second_done)
+        more(1, sig, [(z, y) for z in outer], 2)
+    gather_z(1, sig)
+    for f, y in ((0, 0), (1, HALF - 1)):
+        more(1, sig, [(z, y) for z in outer], 3, second_done)
+        send_face(2, sig2, f)
+    for f, z in ((2, 0), (3, HALF - 1)):
+        more(1, sig, [(z, y) for y in inner], 3, second_done)
         send_face(2, sig2, f)
 
     def last_done(span, value):
@@ -767,17 +813,9 @@
                 keep(fine, slice(at, at + 16), r[16 * s : 16 * s + 16])
 
 
-def unfold_kernel(chans, slots, rows, coarse, sel_h, masks_h, fine_h, coarse_h, sel, masks, fine, kept, sem):
-    loads = [
-        pltpu.make_async_copy(a, b, sem.at[i])
-        for i, (a, b) in enumerate(((sel_h, sel), (masks_h, masks)))
-    ]
-    for c in loads:
-        c.start()
+def unfold_kernel(chans, slots, rows, coarse, sel, masks, fine_h, coarse_h, fine, kept, sem):
     kept[...] = coarse[...]
-    for c in loads:
-        c.wait()
-    stores = [pltpu.make_async_copy(kept, coarse_h, sem.at[2])]
+    stores = [pltpu.make_async_copy(kept, coarse_h, sem.at[0])]
     stores[0].start()
     low64, low32 = masks[0] > 0.5, masks[1] > 0.5
     for g in range(slots // 8):
@@ -791,7 +829,7 @@
             r = dot(x.T, jnp.concatenate([sel[0], sel[1]], axis=1)).astype(BF)
             fine[8 * g : 8 * g + 8, :, 256 * h : 256 * h + 256] = r.reshape(8, chans, 256)
         part = pl.ds(8 * g, 8)
-        stores.append(pltpu.make_async_copy(fine.at[part], fine_h.at[part], sem.at[3 + g]))
+        stores.append(pltpu.make_async_copy(fine.at[part], fine_h.at[part], sem.at[1 + g]))
         stores[-1].start()
     for c in stores:
         c.wait()
@@ -840,31 +878,33 @@
         pltpu.VMEM((n_my, 4, cells // 2, width), F32),
         pltpu.VMEM((n, 2, 128), F32),
         pltpu.VMEM((4, 4, -(-(2 * n_my + 2) // 8) * 8, width), F32),
-        pltpu.VMEM((n_my, cells, coarse_weight.shape[1]), F32),
-        pltpu.VMEM((n_my, cells, coarse_weight.shape[1]), F32),
+        pltpu.VMEM((n_my, 2 * cells, coarse_weight.shape[1]), F32),
+        pltpu.VMEM((n_my, 2 * cells, coarse_weight.shape[1]), F32),
         dma((64,)), dma((3, 4)), dma((3, 4)), dma((n,)), dma((n,)),
         dma((3, n_my)), dma((3, n_my)), dma((n_my,)), dma((n_my,)),
         pltpu.SemaphoreType.REGULAR((max(1, (n_mx - 1).bit_length()), 2)),
     ]
     small = (RZ // 2, RY // 2, RX // 2, width)
-    rows, coarse = pl.pallas_call(
+    held_on = pl.pallas_call(
         functools.partial(level_kernel, slots, chans, cells),
-        out_shape=(pltpu.VMEM((2, total, 128), BF), pltpu.VMEM(small, BF)),
+        out_shape=(
+            pltpu.VMEM((2, total, 128), BF), pltpu.VMEM(small, BF),
+            pltpu.VMEM(sel.shape, BF), pltpu.VMEM(masks.shape, BF),
+        ),
         in_specs=[HBM] * len(ins),
-        out_specs=(VM, VM),
+        out_specs=(VM,) * 4,
         scratch_shapes=scratch,
         compiler_params=pltpu.CompilerParams(collective_id=0, has_side_effects=True),
     )(*ins)
     return pl.pallas_call(
         functools.partial(unfold_kernel, chans, slots),
         out_shape=(sds(features.shape, BF), sds(small, BF)),
-        in_specs=[VM, VM, HBM, HBM],
+        in_specs=[VM] * 4,
         out_specs=(HBM, HBM),
         scratch_shapes=[
-            pltpu.VMEM(sel.shape, BF), pltpu.VMEM(masks.shape, BF), pltpu.VMEM(features.shape, BF),
-            pltpu.VMEM(small, BF), dma((3 + slots // 8,)),
+            pltpu.VMEM(features.shape, BF), pltpu.VMEM(small, BF), dma((1 + slots // 8,)),
         ],
-    )(*[pltpu.with_memory_space_constraint(a, pltpu.VMEM) for a in (rows, coarse)], sel, masks)
+    )(*[pltpu.with_memory_space_constraint(a, pltpu.VMEM) for a in held_on])
 
 
 def solution(mesh):

time: 37.9 us -> 36.4 us (0.960)
  Pallas kernels: 35.8 us -> 34.3 us
    pallas_call x1, Pallas kernels: 3.33 us -> 2.42 us  [local(): pl.pallas_call(functools.partial(unfold_kernel, chans, slots), out_shape=...]
    pallas_call x1, Pallas kernels: 32.5 us -> 31.9 us  [local(): pl.pallas_call(functools.partial(level_kernel, slots, chans, cells), out_...]
where the time goes in v5:
time: 36.4 us; the launch traced here: 35.8 us
  Pallas kernels  34.3 us (94%)
  between operations  1.45 us (4%)
    pallas_call x1, Pallas kernels, local(): pl.pallas_call(functools.partial(level_kernel, slots, chans, cells), out_...  31.9 us
    pallas_call x1, Pallas kernels, local(): pl.pallas_call(functools.partial(unfold_kernel, chans, slots), out_shape=...  2.42 us

profile of v5, /device:TPU:0, one launch (start us, length us, event | category | flops | bytes accessed | tf_op | source)
XLA Modules:
  0.0 35.8 jit_solution(9822442697151057157)
XLA Ops:
  1.3 31.9 %shard_map.149 = (bf16[2,2048,128]{2,1,0:T(8,128)(2,1)S(1)}, bf16[2,2,2,256]{3,2,1,0:T(2,128)(2,1)S(1)}, bf16[2,256,128]{2,1,0:T(8,128)(2,1)S(1)}, bf16[2,32,128]{2,1,0:T(8,128)(2,1)S(1)}) custom-call(s32[1,1]{1,0:T(1,128)} %bitcast.4.counts_h, s32[3,32]{1,0:T(4,128)} %coords_h.1, s32[6,32]{1,0:T(8,128)} %neighbours_h.1, bf16[32,32,512]{2,1,0:T(8,128)(2,1)} %feat_h.1, ...), custom_call_target="tpu_custom_call" | custom-call | tf_op jit(solution)/shard_map/pallas_call | solution.py:888
  33.2 2.4 %shard_map.150 = (bf16[32,32,512]{2,1,0:T(8,128)(2,1)}, bf16[2,2,2,256]{3,2,1,0:T(2,128)(2,1)}) custom-call(bf16[2,2048,128]{2,1,0:T(8,128)(2,1)S(1)} %get-tuple-element.6.rows, bf16[2,2,2,256]{3,2,1,0:T(2,128)(2,1)S(1)} %get-tuple-element.7.coarse, bf16[2,256,128]{2,1,0:T(8,128)(2,1)S(1)} %get-tuple-element.8.sel, ...), custom_call_target="tpu_custom_call" | custom-call | tf_op jit(solution)/shard_map/pallas_call | solution.py:899

commit v6 on v5

--- a/solution.py
+++ b/solution.py
@@ -37,7 +37,7 @@
     for w in range(8):
         vy, vz, vx = w >> 2, w >> 1 & 1, w & 1
         for i in range(32):
-            z, y, x = i // 16 * 2 + vz, i // 4 % 4 * 2 + vy, i % 4 * 2 + vx
+            y, z, x = i // 8 * 2 + vy, i // 4 % 2 * 2 + vz, i % 4 * 2 + vx
             sel[w * 32 + i, (z * SIDE + y) * SIDE + x] = 1
     swap = np.zeros((256, 256))
     for i in range(16):
@@ -204,18 +204,30 @@
                 at = (8 * g + s) * CUBES + 32 * h
                 blocks[0, at : at + 32, :] = m[s][0]
                 blocks[1, at : at + 32, :] = m[s][1]
-    loaded("swap")
-    for z in range(HALF):
+    def cube_rows(slot, y):
+        return [slice(slot * CUBES + 32 * h + 8 * y, slot * CUBES + 32 * h + 8 * y + 8) for h in range(2)]
+
+    def by_cube(y):
         for g in range(slots // 16):
             x = jnp.concatenate(
-                [wide_of(blocks, pl.ds((16 * g + s) * CUBES + 16 * z, 16)) for s in range(16)], axis=0)
+                [wide_of(blocks, span) for s in range(16) for span in cube_rows(16 * g + s, y)], axis=0)
             r = dot(pair_of(swap), x)
             rb = r.astype(BF)
             rs = silu(r).astype(BF)
             for i in range(16):
-                at = (16 * z + i) * slots + 16 * g
+                at = ((i // HALF * HALF + y) * HALF + i % HALF) * slots + 16 * g
                 keep(base, slice(at, at + 16), rb[16 * i : 16 * i + 16])
                 keep(sig, slice(at, at + 16), rs[16 * i : 16 * i + 16])
+
+    def by_slot(y):
+        for g in range(slots // 16):
+            x = jnp.concatenate(
+                [wide_of(base, pl.ds(((i // HALF * HALF + y) * HALF + i % HALF) * slots + 16 * g, 16))
+                 for i in range(16)], axis=0)
+            r = dot(pair_of(swap), x).astype(BF)
+            for s in range(16):
+                for h, span in enumerate(cube_rows(16 * g + s, y)):
+                    keep(fine, span, r[16 * s + 8 * h : 16 * s + 8 * h + 8])
 
     loaded("counts", "coords", "neighbours")
     def one_hot(row, count):
@@ -267,17 +279,21 @@
         (mx < n_mx - 1, mx + 1, my),
     )
 
-    def face_copy(r, f):
+    def pieces(r, f):
+        return ((4, 8), (0, 4), (12, 4)) if r == 2 and f < 2 else ((0, PLANE),)
+
+    def face_copy(r, f, i):
         _, a, b = peers[f]
+        span = pl.ds(*pieces(r, f)[i])
         return pltpu.make_async_remote_copy(
-            src_ref=faces.at[r, f], dst_ref=halo.at[r, f], send_sem=fsend.at[r, f],
-            recv_sem=frecv.at[r, f], device_id=(a, b), device_id_type=MESH,
+            src_ref=faces.at[r, f, span], dst_ref=halo.at[r, f, span], send_sem=fsend.at[r, f, i],
+            recv_sem=frecv.at[r, f, i], device_id=(a, b), device_id_type=MESH,
         )
 
     low64_face = low64[:FACE]
 
-    def send_face(r, src, f):
-        for k in range(PLANE // 2):
+    def send_face(r, src, f, zs=range(HALF), sent=(0,)):
+        for k in [2 * z + i for z in zs for i in range(2)]:
             a, x = k // 2, k % 2 * 2
             if f < 2:
                 part_of = left if f == 0 else right
@@ -300,22 +316,26 @@
 
         @pl.when(peers[f][0])
         def _():
-            face_copy(r, f).start()
-
-        @pl.when(jnp.logical_not(peers[f ^ 1][0]))
-        def _():
-            halo[r, f] = jnp.zeros_like(halo[r, f])
+            for i in sent:
+                face_copy(r, f, i).start()
+
+        if 0 in sent:
+            @pl.when(jnp.logical_not(peers[f ^ 1][0]))
+            def _():
+                halo[r, f] = jnp.zeros_like(halo[r, f])
 
     def sent_faces(r):
         for f in range(4):
             @pl.when(peers[f][0])
             def _():
-                face_copy(r, f).wait_send()
+                for i in range(len(pieces(r, f))):
+                    face_copy(r, f, i).wait_send()
 
     def take_face(r, f):
         @pl.when(peers[f ^ 1][0])
         def _():
-            face_copy(r, f).wait_recv()
+            for i in range(len(pieces(r, f))):
+                face_copy(r, f, i).wait_recv()
 
     def z_halo(r, f, y, x):
         k = 2 * (y * 2 + x // 2)
@@ -503,8 +523,15 @@
     def first_done(span, value):
         keep(base, span, value.astype(BF))
 
+    loaded("swap")
+    by_cube(0)
     entered()
-    for f in (0, 1, 2, 3):
+    send_face(0, sig, 0)
+    by_cube(HALF - 1)
+    send_face(0, sig, 1)
+    for y in inner:
+        by_cube(y)
+    for f in (2, 3):
         send_face(0, sig, f)
     if rounds:
         tell(0)
@@ -781,11 +808,12 @@
     for f, y in ((1, 0), (0, HALF - 1)):
         gather_y(1, sig, f)
         more(1, sig, [(z, y) for z in inner], 2, second_done)
+        send_face(2, sig2, f ^ 1, inner)
         more(1, sig, [(z, y) for z in outer], 2)
     gather_z(1, sig)
     for f, y in ((0, 0), (1, HALF - 1)):
         more(1, sig, [(z, y) for z in outer], 3, second_done)
-        send_face(2, sig2, f)
+        send_face(2, sig2, f, outer, (1, 2))
     for f, z in ((2, 0), (3, HALF - 1)):
         more(1, sig, [(z, y) for y in inner], 3, second_done)
         send_face(2, sig2, f)
@@ -799,18 +827,12 @@
     near_outer(2, sig2)
     far_z(2, sig2, last_done)
     sent_faces(1)
-    for f in (1, 0):
+    for y in inner:
+        by_slot(y)
+    for f, y in ((1, 0), (0, HALF - 1)):
         far_y(2, sig2, last_done, f)
-
+        by_slot(y)
     sent_faces(2)
-    for g in range(slots // 16):
-        for z in range(HALF):
-            x = jnp.concatenate(
-                [wide_of(base, pl.ds((16 * z + i) * slots + 16 * g, 16)) for i in range(16)], axis=0)
-            r = dot(pair_of(swap), x).astype(BF)
-            for s in range(16):
-                at = (16 * g + s) * CUBES + 16 * z
-                keep(fine, slice(at, at + 16), r[16 * s : 16 * s + 16])
 
 
 def unfold_kernel(chans, slots, rows, coarse, sel, masks, fine_h, coarse_h, fine, kept, sem):
@@ -880,7 +902,7 @@
         pltpu.VMEM((4, 4, -(-(2 * n_my + 2) // 8) * 8, width), F32),
         pltpu.VMEM((n_my, 2 * cells, coarse_weight.shape[1]), F32),
         pltpu.VMEM((n_my, 2 * cells, coarse_weight.shape[1]), F32),
-        dma((64,)), dma((3, 4)), dma((3, 4)), dma((n,)), dma((n,)),
+        dma((64,)), dma((3, 4, 3)), dma((3, 4, 3)), dma((n,)), dma((n,)),
         dma((3, n_my)), dma((3, n_my)), dma((n_my,)), dma((n_my,)),
         pltpu.SemaphoreType.REGULAR((max(1, (n_mx - 1).bit_length()), 2)),
     ]

time: 36.4 us -> 37 us (1.016)
  Pallas kernels: 34.3 us -> 35.2 us
    pallas_call x1, Pallas kernels: 31.9 us -> 32.8 us  [local(): pl.pallas_call(functools.partial(level_kernel, slots, chans, cells), out_...]
where the time goes in v6:
time: 37 us; the launch traced here: 36.7 us
  Pallas kernels  35.2 us (95%)
  between operations  1.45 us (4%)
    pallas_call x1, Pallas kernels, local(): pl.pallas_call(functools.partial(level_kernel, slots, chans, cells), out_...  32.8 us
    pallas_call x1, Pallas kernels, local(): pl.pallas_call(functools.partial(unfold_kernel, chans, slots), out_shape=...  2.42 us

profile of v6, /device:TPU:0, one launch (start us, length us, event | category | flops | bytes accessed | tf_op | source)
XLA Modules:
  0.0 36.7 jit_solution(7275592401543881936)
XLA Ops:
  1.3 32.8 %shard_map.149 = (bf16[2,2048,128]{2,1,0:T(8,128)(2,1)S(1)}, bf16[2,2,2,256]{3,2,1,0:T(2,128)(2,1)S(1)}, bf16[2,256,128]{2,1,0:T(8,128)(2,1)S(1)}, bf16[2,32,128]{2,1,0:T(8,128)(2,1)S(1)}) custom-call(s32[1,1]{1,0:T(1,128)} %bitcast.4.counts_h, s32[3,32]{1,0:T(4,128)} %coords_h.1, s32[6,32]{1,0:T(8,128)} %neighbours_h.1, bf16[32,32,512]{2,1,0:T(8,128)(2,1)} %feat_h.1, ...), custom_call_target="tpu_custom_call" | custom-call | tf_op jit(solution)/shard_map/pallas_call | solution.py:910
  34.1 2.4 %shard_map.150 = (bf16[32,32,512]{2,1,0:T(8,128)(2,1)}, bf16[2,2,2,256]{3,2,1,0:T(2,128)(2,1)}) custom-call(bf16[2,2048,128]{2,1,0:T(8,128)(2,1)S(1)} %get-tuple-element.6.rows, bf16[2,2,2,256]{3,2,1,0:T(2,128)(2,1)S(1)} %get-tuple-element.7.coarse, bf16[2,256,128]{2,1,0:T(8,128)(2,1)S(1)} %get-tuple-element.8.sel, ...), custom_call_target="tpu_custom_call" | custom-call | tf_op jit(solution)/shard_map/pallas_call | solution.py:921

commit v7 on v5

--- a/solution.py
+++ b/solution.py
@@ -520,9 +520,7 @@
     if rounds < 2:
         far_z(0, sig, first_done)
     far_y(0, sig, first_done, 1)
-    send_face(1, base, 0)
     far_y(0, sig, first_done, 0)
-    send_face(1, base, 1)
 
     sums = []
     for o in range(8):
@@ -614,6 +612,8 @@
         @pl.when(high)
         def _():
             win_copy(2, d).start()
+    for f in range(2):
+        send_face(1, base, f)
     window[my, 1:3] = coarse[...]
     everyone[me] = stats[...]
 

time: 36.4 us -> 36.1 us (level)
  no operation moved by 1% of the time
where the time goes in v7:
time: 36.1 us; the launch traced here: 35.4 us
  Pallas kernels  34 us (94%)
  between operations  1.45 us (4%)
    pallas_call x1, Pallas kernels, local(): pl.pallas_call(functools.partial(level_kernel, slots, chans, cells), out_...  31.6 us
    pallas_call x1, Pallas kernels, local(): pl.pallas_call(functools.partial(unfold_kernel, chans, slots), out_shape=...  2.42 us

profile of v7, /device:TPU:0, one launch (start us, length us, event | category | flops | bytes accessed | tf_op | source)
XLA Modules:
  0.0 35.4 jit_solution(12537077424628262563)
XLA Ops:
  1.3 31.6 %shard_map.149 = (bf16[2,2048,128]{2,1,0:T(8,128)(2,1)S(1)}, bf16[2,2,2,256]{3,2,1,0:T(2,128)(2,1)S(1)}, bf16[2,256,128]{2,1,0:T(8,128)(2,1)S(1)}, bf16[2,32,128]{2,1,0:T(8,128)(2,1)S(1)}) custom-call(s32[1,1]{1,0:T(1,128)} %bitcast.4.counts_h, s32[3,32]{1,0:T(4,128)} %coords_h.1, s32[6,32]{1,0:T(8,128)} %neighbours_h.1, bf16[32,32,512]{2,1,0:T(8,128)(2,1)} %feat_h.1, ...), custom_call_target="tpu_custom_call" | custom-call | tf_op jit(solution)/shard_map/pallas_call | solution.py:888
  32.8 2.4 %shard_map.150 = (bf16[32,32,512]{2,1,0:T(8,128)(2,1)}, bf16[2,2,2,256]{3,2,1,0:T(2,128)(2,1)}) custom-call(bf16[2,2048,128]{2,1,0:T(8,128)(2,1)S(1)} %get-tuple-element.6.rows, bf16[2,2,2,256]{3,2,1,0:T(2,128)(2,1)S(1)} %get-tuple-element.7.coarse, bf16[2,256,128]{2,1,0:T(8,128)(2,1)S(1)} %get-tuple-element.8.sel, ...), custom_call_target="tpu_custom_call" | custom-call | tf_op jit(solution)/shard_map/pallas_call | solution.py:899

commit v8 on v7

--- a/solution.py
+++ b/solution.py
@@ -103,13 +103,13 @@
 
     chunks = feat.shape[0]
     order = [
+        ("counts", counts_h, counts), ("coords", coords_h, coords),
+        ("neighbours", neighbours_h, neighbours), ("fine_w", fine_w_h, fine_w),
+    ]
+    order += [
         ("feat", feat_h.at[:, :, pl.ds(128 * k, 128)], feat.at[k]) for k in range(chunks)
     ]
-    order += [
-        ("sel", sel_h, sel), ("masks", masks_h, masks), ("swap", swap_h, swap),
-        ("fine_w", fine_w_h, fine_w), ("counts", counts_h, counts),
-        ("coords", coords_h, coords), ("neighbours", neighbours_h, neighbours),
-    ]
+    order += [("sel", sel_h, sel), ("masks", masks_h, masks), ("swap", swap_h, swap)]
     late = [("same", same_h, same), ("gain", gain_h, gain), ("bias", bias_h, bias)]
     late += [("down", down_h.at[:, pl.ds(128 * k, 128)], down.at[k]) for k in range(down.shape[0])]
     late += [("weight", weight_h, weight)]
@@ -169,6 +169,80 @@
         @pl.when(mx + 2**k < n_mx)
         def _():
             pl.semaphore_wait(ready.at[k, 1], 1)
+
+    loaded("counts", "coords", "neighbours")
+    def one_hot(row, count):
+        return (lax.broadcasted_iota(I32, (count, slots), 0) == row).astype(F32).astype(BF)
+
+    eye = (
+        lax.broadcasted_iota(I32, (slots, slots), 0) == lax.broadcasted_iota(I32, (slots, slots), 1)
+    ).astype(F32).astype(BF)
+
+    def turned(table):
+        return dot(eye, table, NT).astype(BF)
+
+    pz = coords[0:1, :] - mx * RZ
+    py = coords[1:2, :] - my * RY
+    px = coords[2:3, :]
+    live = lax.broadcasted_iota(I32, (1, slots), 1) < counts[...]
+
+    def link(d):
+        g = neighbours[d : d + 1, :]
+        here = g - me * slots
+        inside = (here >= 0) & (here < slots)
+        far = slots + (pz if d < 4 else py) * RX + px
+        return jnp.where(g < 0, -1, jnp.where(inside, here, far))
+
+    halo_rows = slots + FACE
+    g_x = turned(jnp.concatenate([one_hot(link(d), slots) for d in (0, 1)], axis=0))
+    g_yp = turned(one_hot(link(2), halo_rows))
+    g_ym = turned(one_hot(link(3), halo_rows))
+    g_z = turned(jnp.concatenate([one_hot(link(d), halo_rows) for d in (4, 5)], axis=0))
+    edge = (
+        jnp.where(live & (py == 0), pz * RX + px, -1),
+        jnp.where(live & (py == RY - 1), pz * RX + px, -1),
+        jnp.where(live & (pz == 0), py * RX + px, -1),
+        jnp.where(live & (pz == RZ - 1), py * RX + px, -1),
+    )
+    g_edge = [one_hot(e, FACE) for e in edge]
+    cell = (pz // 2 * 2 + px // 2) * 2 + py // 2
+    place = pz % 2 * 4 + py % 2 * 2 + px % 2
+    g_cell = one_hot(jnp.where(live, place * cells + cell, -1), 8 * cells)
+    g_lift = turned(g_cell)
+    alive = dot(
+        jnp.where(live, eye.astype(F32), 0.0).astype(BF), jnp.ones((slots, width), BF)
+    ) > 0.5
+
+    lane_block = lax.broadcasted_iota(I32, (slots, width), 1) // chans
+    block_f = lane_block.astype(F32).astype(BF)
+    spread = (
+        lax.broadcasted_iota(I32, (chans, width), 0)
+        == lax.broadcasted_iota(I32, (chans, width), 1) % chans
+    ).astype(F32).astype(BF)
+    none = jnp.zeros((chans, width), BF)
+    is_block = [block_f == float(w) for w in range(8)]
+
+    def fit(r, k, span, v):
+        for t in range(2):
+            wts[r, k, t, span, :] = v[:, side * t : side * t + side]
+
+    def fill(r):
+        t = dot(fine_w[r], spread, TN).astype(BF)
+        t = [t[i * chans : (i + 1) * chans] for i in range(7)]
+        for w in range(8):
+            span = slice(w * chans, (w + 1) * chans)
+            vy, vz, vx = w >> 2, w >> 1 & 1, w & 1
+            v = jnp.where(is_block[w], t[0], none)
+            v = jnp.where(is_block[w ^ 1], t[1] if vx else t[2], v)
+            v = jnp.where(is_block[w ^ 4], t[3] if vy else t[4], v)
+            v = jnp.where(is_block[w ^ 2], t[5] if vz else t[6], v)
+            fit(r, 0, span, v)
+            fit(r, 1, span, jnp.where(is_block[w ^ 1], t[2] if vx else t[1], none))
+            fit(r, 2, span, jnp.where(is_block[w ^ 4], t[4] if vy else t[3], none))
+            fit(r, 3, span, jnp.where(is_block[w ^ 2], t[6] if vz else t[5], none))
+
+    loaded("fine_w")
+    fill(0)
 
     loaded("feat", "sel", "masks")
     for _, c in copies[len(order) :]:
@@ -217,49 +291,6 @@
                 keep(base, slice(at, at + 16), rb[16 * i : 16 * i + 16])
                 keep(sig, slice(at, at + 16), rs[16 * i : 16 * i + 16])
 
-    loaded("counts", "coords", "neighbours")
-    def one_hot(row, count):
-        return (lax.broadcasted_iota(I32, (count, slots), 0) == row).astype(F32).astype(BF)
-
-    eye = (
-        lax.broadcasted_iota(I32, (slots, slots), 0) == lax.broadcasted_iota(I32, (slots, slots), 1)
-    ).astype(F32).astype(BF)
-
-    def turned(table):
-        return dot(eye, table, NT).astype(BF)
-
-    pz = coords[0:1, :] - mx * RZ
-    py = coords[1:2, :] - my * RY
-    px = coords[2:3, :]
-    live = lax.broadcasted_iota(I32, (1, slots), 1) < counts[...]
-
-    def link(d):
-        g = neighbours[d : d + 1, :]
-        here = g - me * slots
-        inside = (here >= 0) & (here < slots)
-        far = slots + (pz if d < 4 else py) * RX + px
-        return jnp.where(g < 0, -1, jnp.where(inside, here, far))
-
-    halo_rows = slots + FACE
-    g_x = turned(jnp.concatenate([one_hot(link(d), slots) for d in (0, 1)], axis=0))
-    g_yp = turned(one_hot(link(2), halo_rows))
-    g_ym = turned(one_hot(link(3), halo_rows))
-    g_z = turned(jnp.concatenate([one_hot(link(d), halo_rows) for d in (4, 5)], axis=0))
-    edge = (
-        jnp.where(live & (py == 0), pz * RX + px, -1),
-        jnp.where(live & (py == RY - 1), pz * RX + px, -1),
-        jnp.where(live & (pz == 0), py * RX + px, -1),
-        jnp.where(live & (pz == RZ - 1), py * RX + px, -1),
-    )
-    g_edge = [one_hot(e, FACE) for e in edge]
-    cell = (pz // 2 * 2 + px // 2) * 2 + py // 2
-    place = pz % 2 * 4 + py % 2 * 2 + px % 2
-    g_cell = one_hot(jnp.where(live, place * cells + cell, -1), 8 * cells)
-    g_lift = turned(g_cell)
-    alive = dot(
-        jnp.where(live, eye.astype(F32), 0.0).astype(BF), jnp.ones((slots, width), BF)
-    ) > 0.5
-
     peers = (
         (my > 0, mx, my - 1),
         (my < n_my - 1, mx, my + 1),
@@ -472,34 +503,6 @@
         for zs in (range(HALF // 2), range(HALF // 2, HALF)):
             more(r, src, [(z, y) for z in zs], 2, finish)
 
-    lane_block = lax.broadcasted_iota(I32, (slots, width), 1) // chans
-    block_f = lane_block.astype(F32).astype(BF)
-    spread = (
-        lax.broadcasted_iota(I32, (chans, width), 0)
-        == lax.broadcasted_iota(I32, (chans, width), 1) % chans
-    ).astype(F32).astype(BF)
-    none = jnp.zeros((chans, width), BF)
-    is_block = [block_f == float(w) for w in range(8)]
-
-    def fit(r, k, span, v):
-        for t in range(2):
-            wts[r, k, t, span, :] = v[:, side * t : side * t + side]
-
-    def fill(r):
-        t = dot(fine_w[r], spread, TN).astype(BF)
-        t = [t[i * chans : (i + 1) * chans] for i in range(7)]
-        for w in range(8):
-            span = slice(w * chans, (w + 1) * chans)
-            vy, vz, vx = w >> 2, w >> 1 & 1, w & 1
-            v = jnp.where(is_block[w], t[0], none)
-            v = jnp.where(is_block[w ^ 1], t[1] if vx else t[2], v)
-            v = jnp.where(is_block[w ^ 4], t[3] if vy else t[4], v)
-            v = jnp.where(is_block[w ^ 2], t[5] if vz else t[6], v)
-            fit(r, 0, span, v)
-            fit(r, 1, span, jnp.where(is_block[w ^ 1], t[2] if vx else t[1], none))
-            fit(r, 2, span, jnp.where(is_block[w ^ 4], t[4] if vy else t[3], none))
-            fit(r, 3, span, jnp.where(is_block[w ^ 2], t[6] if vz else t[5], none))
-
     def first_done(span, value):
         keep(base, span, value.astype(BF))
 
@@ -508,17 +511,15 @@
         send_face(0, sig, f)
     if rounds:
         tell(0)
-    loaded("fine_w")
-    fill(0)
     near_inner(0, sig, first_done)
+    if rounds > 1:
+        hear(0)
+        tell(1)
     near_outer(0, sig)
-    for k in range(1, rounds):
+    for k in range(2, rounds):
         hear(k - 1)
         tell(k)
-        if k == 1:
-            far_z(0, sig, first_done)
-    if rounds < 2:
-        far_z(0, sig, first_done)
+    far_z(0, sig, first_done)
     far_y(0, sig, first_done, 1)
     far_y(0, sig, first_done, 0)
 
@@ -657,11 +658,11 @@
     both_rows = jnp.concatenate([mean, std, jnp.zeros((6, lanes), F32)], axis=0)
     both_rows = in_three(both_rows, grouped, NT)
     mean, std = both_rows[0:1], both_rows[1:2]
-    g = gain[...]
-    b = bias[...]
+    scale = gain[...] / std
+    shift = bias[...] - mean * scale
     for zw in range(4):
         for j in range(n_my):
-            value = silu((window[j, zw] - mean) / std * g + b)
+            value = silu(window[j, zw] * scale + shift)
             if zw == 0:
                 value = jnp.where(low, value, 0.0)
             if zw == 3:

time: 36.1 us -> 35.9 us (level)
  no operation moved by 1% of the time
where the time goes in v8:
time: 35.9 us; the launch traced here: 35.3 us
  Pallas kernels  33.8 us (94%)
  between operations  1.45 us (4%)
    pallas_call x1, Pallas kernels, local(): pl.pallas_call(functools.partial(level_kernel, slots, chans, cells), out_...  31.4 us
    pallas_call x1, Pallas kernels, local(): pl.pallas_call(functools.partial(unfold_kernel, chans, slots), out_shape=...  2.42 us

profile of v8, /device:TPU:0, one launch (start us, length us, event | category | flops | bytes accessed | tf_op | source)
XLA Modules:
  0.0 35.3 jit_solution(3232619527083697989)
XLA Ops:
  1.3 31.4 %shard_map.149 = (bf16[2,2048,128]{2,1,0:T(8,128)(2,1)S(1)}, bf16[2,2,2,256]{3,2,1,0:T(2,128)(2,1)S(1)}, bf16[2,256,128]{2,1,0:T(8,128)(2,1)S(1)}, bf16[2,32,128]{2,1,0:T(8,128)(2,1)S(1)}) custom-call(s32[1,1]{1,0:T(1,128)} %bitcast.4.counts_h, s32[3,32]{1,0:T(4,128)} %coords_h.1, s32[6,32]{1,0:T(8,128)} %neighbours_h.1, bf16[32,32,512]{2,1,0:T(8,128)(2,1)} %feat_h.1, ...), custom_call_target="tpu_custom_call" | custom-call | tf_op jit(solution)/shard_map/pallas_call | solution.py:889
  32.7 2.4 %shard_map.150 = (bf16[32,32,512]{2,1,0:T(8,128)(2,1)}, bf16[2,2,2,256]{3,2,1,0:T(2,128)(2,1)}) custom-call(bf16[2,2048,128]{2,1,0:T(8,128)(2,1)S(1)} %get-tuple-element.6.rows, bf16[2,2,2,256]{3,2,1,0:T(2,128)(2,1)S(1)} %get-tuple-element.7.coarse, bf16[2,256,128]{2,1,0:T(8,128)(2,1)S(1)} %get-tuple-element.8.sel, ...), custom_call_target="tpu_custom_call" | custom-call | tf_op jit(solution)/shard_map/pallas_call | solution.py:900
